TPU v7x, 128 devices: a whole 4x4x4 slice. The times are simulated.
128 devices in a mesh: slab: 16 (over x, y_hi, core), tile: 8 (over y_lo, z).
Axes of the slice: x: 4, y: 4 (y_hi: 2, y_lo: 2; y = y_hi * 2 + y_lo), z: 4, core: 2. Of those that a mesh axis runs over, the one named last changes fastest.
Arguments:
- velocity: float32 [3, 512, 128, 128], P(None, 'slab', 'tile'), may hold values from -4 to 4
- viscosity: float32 [512, 128, 128], P('slab', 'tile'), may hold values from 0.2 to 0.6
- basis: bfloat16 [32, 3, 512, 128, 128], P(None, None, ('slab', 'tile')), may hold values from -6 to 6
- sigma: float32 [32], replicated, may hold values from 0.3 to 3
- rotation: float32 [35, 32], replicated, may hold values from -1 to 1
Outputs:
- advanced: float32 [3, 512, 128, 128], P(None, 'slab', 'tile')
- r_factor: float32 [35, 35], replicated
- new_basis: bfloat16 [32, 3, 512, 128, 128], P(None, None, ('slab', 'tile'))
All inputs are finite; a program needn't handle non-finite values.
Results may differ from a plain program's by a relative error of at most 0.001.
Values sent between devices are 32-bit elements; how exact they have to be, the bound alone decides.
A program may use at most 256 MiB of HBM per device.

v0:
```python
import math

import jax
import jax.numpy as jnp
from jax import lax
from jax.sharding import PartitionSpec as P

step_size = 0.25


def extended(block, sides, width):
    for axis, dim in sides:
        count = lax.axis_size(axis)
        forward = [(i, i + 1) for i in range(count - 1)]
        forward.append((count - 1, 0))
        backward = [(target, source) for source, target in forward]
        low = lax.ppermute(
            lax.slice_in_dim(block, block.shape[dim] - width, None, axis=dim), axis, forward
        )
        high = lax.ppermute(lax.slice_in_dim(block, 0, width, axis=dim), axis, backward)
        block = jnp.concatenate([low, block, high], axis=dim)
    return block


def upper_factor(gram):
    order = gram.shape[0]
    positions = jnp.arange(order)
    factor = jnp.zeros_like(gram)
    for column_index in range(order):
        above = factor[:, column_index]
        remainder = gram[column_index] - jnp.dot(
            above, factor, precision=lax.Precision.HIGHEST, preferred_element_type=jnp.float32
        )
        pivot = jnp.sqrt(remainder[column_index])
        new_row = jnp.where(positions >= column_index, remainder / pivot, 0.0)
        factor = factor.at[column_index].set(new_row)
    return factor


def upper_solve(factor, right_hand):
    order = factor.shape[0]
    solved = jnp.zeros_like(right_hand)
    for row_index in range(order - 1, -1, -1):
        partial_sum = jnp.dot(
            factor[row_index],
            solved,
            precision=lax.Precision.HIGHEST,
            preferred_element_type=jnp.float32,
        )
        solved = solved.at[row_index].set(
            (right_hand[row_index] - partial_sum) / factor[row_index, row_index]
        )
    return solved


def advance(padded, viscosity):
    centre = padded[:, 1:-1, 1:-1, :]
    forward_x = padded[:, 2:, 1:-1, :]
    backward_x = padded[:, :-2, 1:-1, :]
    forward_z = padded[:, 1:-1, 2:, :]
    backward_z = padded[:, 1:-1, :-2, :]
    walled = jnp.pad(centre, ((0, 0), (0, 0), (0, 0), (1, 1)))
    above_y = walled[..., 2:]
    below_y = walled[..., :-2]
    laplace = forward_x + backward_x + forward_z + backward_z + above_y + below_y - 6.0 * centre
    carried = (
        centre[0:1] * (forward_x - backward_x)
        + centre[1:2] * (above_y - below_y)
        + centre[2:3] * (forward_z - backward_z)
    )
    return centre + step_size * (viscosity * laplace - 0.5 * carried)


def shards(velocity, viscosity, basis, sigma, rotation):
    current = velocity
    history = [velocity]
    for repeat in range(2):
        padded = extended(current, (("slab", 1), ("tile", 2)), 1)
        current = advance(padded, viscosity)
        history.append(current)
    snapshots = lax.all_to_all(jnp.stack(history), "tile", split_axis=2, concat_axis=3, tiled=True)
    strip_width = basis.shape[2]
    row_count = (
        3
        * strip_width
        * lax.axis_size("slab")
        * lax.axis_size("tile")
        * basis.shape[3]
        * basis.shape[4]
    )
    row_scale = math.sqrt(row_count)
    width_all = sigma.shape[0] + 3
    scaled = basis.astype(jnp.float32) * sigma[:, None, None, None, None]
    columns = jnp.concatenate([scaled, snapshots], 0).reshape(width_all, -1)
    local_gram = jnp.dot(
        columns, columns.T, precision=lax.Precision.HIGHEST, preferred_element_type=jnp.float32
    )
    gram = lax.psum(local_gram, ("slab", "tile"))
    factor = upper_factor(gram)
    mixing = upper_solve(factor, rotation) * row_scale
    rotated = jnp.dot(
        mixing.T, columns, precision=lax.Precision.HIGHEST, preferred_element_type=jnp.float32
    )
    rotated = rotated.reshape(basis.shape).astype(jnp.bfloat16)
    return (current, factor / row_scale, rotated)


def solution(mesh):
    in_specs = (
        P(None, "slab", "tile", None),
        P("slab", "tile", None),
        P(None, None, ("slab", "tile"), None, None),
        P(),
        P(),
    )
    out_specs = (P(None, "slab", "tile", None), P(), P(None, None, ("slab", "tile"), None, None))
    return jax.shard_map(shards, mesh=mesh, in_specs=in_specs, out_specs=out_specs, check_vma=False)
```

profile of v0, /device:TPU:1, one launch (start us, length us, event | category | flops | bytes accessed | tf_op | source)
XLA Modules:
  0.0 461.0 jit_solution(1416673244914366114)
XLA Ops:
  1.4 4.3 collective-permute-start.1
  6.7 1.2 copy_bitcast_fusion.1
  7.9 2.6 collective-permute-done
  10.5 3.9 collective-permute-start.2
  14.5 1.2 slice_bitcast_fusion.5
  15.6 1.2 copy.42
  16.8 2.7 collective-permute-done.3
  19.6 1.8 multiply_add_fusion.1
  21.4 3.4 collective-permute-start.5
  25.7 4.1 collective-permute-done.4
  30.0 1.5 collective-permute-start.7
  31.5 1.4 collective-permute-done.6
  32.9 2.2 collective-permute-done.7
  35.1 1.8 fusion.306
  36.9 1.6 pad_maximum_fusion.1
  38.6 3.8 all-to-all-start
  42.4 11.8 %convert_multiply_fusion = f32[32,3,4,128,128]{4,0,3,2,1:T(8,128)S(1)} fusion(bf16[32,3,4,128,128]{4,3,2,1,0:T(8,128)(2,1)} %param.147, f32[32]{0:T(128)} %param.148), kind=kLoop, calls=%fused_computation.8 | loop fusion | flops 12582912 | bytes 37748864 | tf_op jit(solution)/shard_map/mul | solution.py:93
  54.1 28.1 %copy.82 = f32[32,3,4,128,128]{4,3,2,1,0:T(8,128)} copy(f32[32,3,4,128,128]{4,0,3,2,1:T(8,128)S(1)} %convert_multiply_fusion) | data formatting | bytes 50331648 | tf_op jit(solution)/shard_map/mul | solution.py:93
  82.3 25.1 %copy.100 = f32[4,8,1536,128]{3,1,2,0:T(8,128)} copy(f32[4,8,1536,128]{3,2,1,0:T(8,128)} %bitcast.1128) | data formatting | bytes 50331648
  107.4 1.0 slice_reduce_fusion.35
  108.5 1.1 slice_reduce_fusion.34
  110.7 0.9 copy.84
  111.6 1.4 copy-done.3
  113.0 3.0 copy.46
  116.0 28.8 %fusion.9 = f32[35,35]{1,0:T(8,128)S(1)} fusion(f32[3,3,4,128,128]{4,0,3,2,1:T(4,128)S(1)} %bitcast.1130, f32[32,3,4,128,128]{4,0,3,2,1:T(8,128)} %copy-done.1), kind=kOutput, calls=%fused_computation.15 | convolution fusion | flops 2897018880 | bytes 27530020 | tf_op jit(solution)/shard_map/dot_general | solution.py:95
  144.8 68.9 %psum.7 = f32[35,35]{1,0:T(8,128)S(1)} all-reduce(f32[35,35]{1,0:T(8,128)S(1)} %fusion.9), channel_id=1, replica_groups=mesh['slab'=16,'tile'=8] {'slab','tile'}, use_global_device_ids=true, to_apply=%region_0.1 | all-reduce | flops 1225 | bytes 9800 | tf_op jit(solution)/shard_map/psum | solution.py:98
  298.0 1.4 fusion.87
  299.7 1.5 fusion.89
  301.4 1.4 fusion.91
  303.0 1.4 fusion.93
  304.7 1.4 fusion.95
  306.4 1.4 fusion.97
  308.1 1.5 fusion.99
  309.9 1.4 fusion.101
  311.6 1.4 fusion.103
  313.2 1.5 fusion.105
  315.0 1.4 fusion.107
  316.6 1.5 fusion.109
  318.3 1.4 fusion.111
  320.0 1.4 fusion.113
  321.7 1.4 fusion.115
  323.3 1.5 fusion.117
  325.1 1.4 fusion.119
  326.7 1.4 fusion.121
  328.4 1.4 fusion.123
  330.0 1.4 fusion.125
  331.7 1.5 fusion.127
  333.4 1.5 fusion.129
  335.2 1.4 fusion.131
  336.8 1.5 fusion.133
  338.6 1.4 fusion.135
  340.3 1.4 fusion.137
  342.0 1.4 fusion.139
  343.7 1.4 fusion.141
  345.3 1.5 fusion.143
  347.0 1.4 fusion.145
  348.6 1.4 fusion.147
  350.3 1.4 fusion.149
  352.0 1.4 fusion.151
  353.6 10.1 %pad_maximum_fusion = f32[35,196608]{1,0:T(8,128)S(1)} fusion(f32[3,196608]{1,0:T(4,128)S(1)} %bitcast.1131, f32[32,196608]{1,0:T(8,128)} %bitcast.1127), kind=kLoop, calls=%fused_computation.4 | loop fusion | flops 6881280 | bytes 55050240 | tf_op jit(solution)/shard_map/concatenate | solution.py:94
  363.7 14.4 %copy.89 = f32[5,8,1536,128]{3,2,1,0:T(8,128)} copy(f32[5,8,1536,128]{3,1,2,0:T(8,128)S(1)} %bitcast.1125) | data formatting | bytes 62914560
  378.1 20.3 %slice.2142 = f32[35,1536,128]{2,1,0:T(8,128)} slice(f32[40,1536,128]{2,1,0:T(8,128)} %bitcast.1126), slice={[0:35], [0:1536], [0:128]} | slice | bytes 55050240
  398.3 48.0 %fusion.6 = bf16[32,3,4,128,128]{4,0,3,2,1:T(8,128)(2,1)S(1)} fusion(f32[3,4,128,128,35]{3,2,1,0,4:T(8,128)} %bitcast.1124, f32[35,32]{0,1:T(8,128)S(1)} %scatter.349), kind=kOutput, calls=%fused_computation.9 | convolution fusion | flops 2648704000 | bytes 40112512 | tf_op jit(solution)/shard_map/dot_general | solution.py:101
  446.4 14.5 %copy.85 = bf16[32,3,4,128,128]{4,3,2,1,0:T(8,128)(2,1)} copy(bf16[32,3,4,128,128]{4,0,3,2,1:T(8,128)(2,1)S(1)} %fusion.6) | data formatting | bytes 25165824
  (336 shorter events, 71.9 us)
Async XLA Ops:
  1.4 5.3 %collective-permute-start.1 = (f32[3,1,16,128]{3,2,0,1:T(8,128)S(1)}, f32[3,1,16,128]{3,2,0,1:T(8,128)S(1)}, u32[]{:S(2)}, u32[]{:S(2)}) collective-permute-start(f32[3,1,16,128]{3,2,0,1:T(8,128)S(1)} %get-tuple-element.905), channel_id=1, source_target_pairs={{0,8},{8,16},{16,24},{24,32},{32,40},{40,48},{48,56},{56,64},{64,7... | collective-permute-start | bytes 73736 | tf_op jit(solution)/shard_map/ppermute | solution.py:17
  5.7 4.8 %collective-permute-start = (f32[3,1,16,128]{3,2,0,1:T(8,128)S(1)}, f32[3,1,16,128]{3,2,0,1:T(8,128)S(1)}, u32[]{:S(2)}, u32[]{:S(2)}) collective-permute-start(f32[3,1,16,128]{3,2,0,1:T(8,128)S(1)} %get-tuple-element.904), channel_id=1, source_target_pairs={{8,0},{16,8},{24,16},{32,24},{40,32},{48,40},{56,48},{64,56},{72,6... | collective-permute-start | bytes 73736 | tf_op jit(solution)/shard_map/ppermute | solution.py:20
  10.5 6.3 %collective-permute-start.2 = (f32[3,34,1,128]{3,2,0,1:T(1,128)S(1)}, f32[3,34,1,128]{3,2,0,1:T(1,128)S(1)}, u32[]{:S(2)}, u32[]{:S(2)}) collective-permute-start(f32[3,34,1,128]{3,2,0,1:T(1,128)S(1)} %get-tuple-element.892), channel_id=1, source_target_pairs={{1,0},{2,1},{3,2},{4,3},{5,4},{6,5},{7,6},{0,7},{9,8},{10,9},{11,1... | collective-permute-start | bytes 156680 | tf_op jit(solution)/shard_map/ppermute | solution.py:20
  14.5 5.1 %collective-permute-start.3 = (f32[3,34,1,128]{3,2,0,1:T(1,128)S(1)}, f32[3,34,1,128]{3,2,0,1:T(1,128)S(1)}, u32[]{:S(2)}, u32[]{:S(2)}) collective-permute-start(f32[3,34,1,128]{3,2,0,1:T(1,128)S(1)} %get-tuple-element.893), channel_id=1, source_target_pairs={{0,1},{1,2},{2,3},{3,4},{4,5},{5,6},{6,7},{7,0},{8,9},{9,10},{10,1... | collective-permute-start | bytes 156680 | tf_op jit(solution)/shard_map/ppermute | solution.py:17
  21.4 4.3 collective-permute-start.5
  24.8 5.1 %collective-permute-start.4 = (f32[3,1,16,128]{3,2,0,1:T(8,128)S(1)}, f32[3,1,16,128]{3,2,0,1:T(8,128)S(1)}, u32[]{:S(2)}, u32[]{:S(2)}) collective-permute-start(f32[3,1,16,128]{3,2,0,1:T(8,128)S(1)} %get-tuple-element.900), channel_id=1, source_target_pairs={{8,0},{16,8},{24,16},{32,24},{40,32},{48,40},{56,48},{64,56},{72,6... | collective-permute-start | bytes 73736 | tf_op jit(solution)/shard_map/ppermute | solution.py:20
  29.9 3.0 collective-permute-start.6
  30.0 5.2 %collective-permute-start.7 = (f32[3,34,1,128]{3,2,0,1:T(1,128)S(1)}, f32[3,34,1,128]{3,2,0,1:T(1,128)S(1)}, u32[]{:S(2)}, u32[]{:S(2)}) collective-permute-start(f32[3,34,1,128]{3,2,0,1:T(1,128)S(1)} %get-tuple-element.891), channel_id=1, source_target_pairs={{0,1},{1,2},{2,3},{3,4},{4,5},{5,6},{6,7},{7,0},{8,9},{9,10},{10,1... | collective-permute-start | bytes 156680 | tf_op jit(solution)/shard_map/ppermute | solution.py:17
  31.5 7.0 %copy-start.4 = (f32[32,16,128]{2,1,0:T(8,128)}, f32[32,16,128]{2,1,0:T(8,128)S(1)}, u32[]{:S(2)}) copy-start(f32[32,16,128]{2,1,0:T(8,128)S(1)} %get-tuple-element.897) | copy-start | bytes 786436
  31.5 7.0 %copy-start.6 = (f32[32,16,128]{2,1,0:T(8,128)}, f32[32,16,128]{2,1,0:T(8,128)S(1)}, u32[]{:S(2)}) copy-start(f32[32,16,128]{2,1,0:T(8,128)S(1)} %get-tuple-element.898) | copy-start | bytes 786436
  35.1 3.4 copy-start.10
  38.6 73.0 %all-to-all-start = ((f32[3,3,32,16,128]{4,3,1,0,2:T(8,128)}), f32[3,3,32,16,128]{4,3,1,0,2:T(8,128)S(1)}, u32[]{:S(2)}, u32[]{:S(2)}) async-start(f32[3,3,32,16,128]{4,3,1,0,2:T(8,128)} %pad_maximum_fusion.1), calls=%async_computation | async-start | bytes 4718592 | tf_op jit(solution)/shard_map/all_to_all | solution.py:81
  54.1 28.2 %copy-start.1 = (f32[32,3,4,128,128]{4,0,3,2,1:T(8,128)}, f32[32,3,4,128,128]{4,0,3,2,1:T(8,128)S(1)}, u32[]{:S(2)}) copy-start(f32[32,3,4,128,128]{4,0,3,2,1:T(8,128)S(1)} %convert_multiply_fusion) | copy-start | bytes 75497472
  82.3 25.1 %copy-start.2 = (f32[35,32]{0,1:T(8,128)S(1)}, f32[35,32]{0,1:T(8,128)}, u32[]{:S(2)}) copy-start(f32[35,32]{0,1:T(8,128)} %param.149) | copy-start | bytes 13444
  82.3 27.3 %copy-start.5 = (f32[32,16,128]{2,1,0:T(8,128)S(1)}, f32[32,16,128]{2,1,0:T(8,128)}, u32[]{:S(2)}) copy-start(f32[32,16,128]{2,1,0:T(8,128)} %copy-done.4) | copy-start | bytes 786436
  82.3 27.3 %copy-start.7 = (f32[32,16,128]{2,1,0:T(8,128)S(1)}, f32[32,16,128]{2,1,0:T(8,128)}, u32[]{:S(2)}) copy-start(f32[32,16,128]{2,1,0:T(8,128)} %copy-done.6) | copy-start | bytes 786436
  82.3 27.2 %copy-start.8 = (f32[32,16,128]{2,1,0:T(8,128)S(1)}, f32[32,16,128]{2,1,0:T(8,128)}, u32[]{:S(2)}) copy-start(f32[32,16,128]{2,1,0:T(8,128)} %param.146) | copy-start | bytes 786436
  82.3 27.2 %copy-start.11 = (f32[3,34,1,128]{3,2,0,1:T(1,128)S(1)}, f32[3,34,1,128]{3,2,0,1:T(1,128)}, u32[]{:S(2)}) copy-start(f32[3,34,1,128]{3,2,0,1:T(1,128)} %copy-done.10) | copy-start | bytes 156676
  110.4 185.6 %copy-start.35 = (f32[32]{0:T(128)S(1)}, f32[32]{0:T(128)}, u32[]{:S(2)}) copy-start(f32[32]{0:T(128)} %get-tuple-element.889) | copy-start | bytes 388
  110.4 186.4 %copy-start.30 = (f32[32]{0:T(128)S(1)}, f32[32]{0:T(128)}, u32[]{:S(2)}) copy-start(f32[32]{0:T(128)} %get-tuple-element.888) | copy-start | bytes 388
  110.4 187.5 %copy-start.29 = (f32[32]{0:T(128)S(1)}, f32[32]{0:T(128)}, u32[]{:S(2)}) copy-start(f32[32]{0:T(128)} %get-tuple-element.887) | copy-start | bytes 388
  110.4 189.2 %copy-start.34 = (f32[32]{0:T(128)S(1)}, f32[32]{0:T(128)}, u32[]{:S(2)}) copy-start(f32[32]{0:T(128)} %get-tuple-element.886) | copy-start | bytes 388
  110.5 191.0 %copy-start.28 = (f32[32]{0:T(128)S(1)}, f32[32]{0:T(128)}, u32[]{:S(2)}) copy-start(f32[32]{0:T(128)} %get-tuple-element.885) | copy-start | bytes 388
  110.5 192.6 %copy-start.27 = (f32[32]{0:T(128)S(1)}, f32[32]{0:T(128)}, u32[]{:S(2)}) copy-start(f32[32]{0:T(128)} %get-tuple-element.884) | copy-start | bytes 388
  110.5 194.3 %copy-start.26 = (f32[32]{0:T(128)S(1)}, f32[32]{0:T(128)}, u32[]{:S(2)}) copy-start(f32[32]{0:T(128)} %get-tuple-element.883) | copy-start | bytes 388
  110.5 196.0 %copy-start.25 = (f32[32]{0:T(128)S(1)}, f32[32]{0:T(128)}, u32[]{:S(2)}) copy-start(f32[32]{0:T(128)} %get-tuple-element.882) | copy-start | bytes 388
  110.5 197.6 %copy-start.24 = (f32[32]{0:T(128)S(1)}, f32[32]{0:T(128)}, u32[]{:S(2)}) copy-start(f32[32]{0:T(128)} %get-tuple-element.881) | copy-start | bytes 388
  110.5 199.4 %copy-start.23 = (f32[32]{0:T(128)S(1)}, f32[32]{0:T(128)}, u32[]{:S(2)}) copy-start(f32[32]{0:T(128)} %get-tuple-element.880) | copy-start | bytes 388
  110.5 201.1 %copy-start.22 = (f32[32]{0:T(128)S(1)}, f32[32]{0:T(128)}, u32[]{:S(2)}) copy-start(f32[32]{0:T(128)} %get-tuple-element.879) | copy-start | bytes 388
  110.5 202.7 %copy-start.33 = (f32[32]{0:T(128)S(1)}, f32[32]{0:T(128)}, u32[]{:S(2)}) copy-start(f32[32]{0:T(128)} %get-tuple-element.878) | copy-start | bytes 388
  110.5 204.4 %copy-start.21 = (f32[32]{0:T(128)S(1)}, f32[32]{0:T(128)}, u32[]{:S(2)}) copy-start(f32[32]{0:T(128)} %get-tuple-element.877) | copy-start | bytes 388
  110.5 206.1 %copy-start.20 = (f32[32]{0:T(128)S(1)}, f32[32]{0:T(128)}, u32[]{:S(2)}) copy-start(f32[32]{0:T(128)} %get-tuple-element.876) | copy-start | bytes 388
  110.6 207.8 %copy-start.19 = (f32[32]{0:T(128)S(1)}, f32[32]{0:T(128)}, u32[]{:S(2)}) copy-start(f32[32]{0:T(128)} %get-tuple-element.875) | copy-start | bytes 388
  110.6 209.5 %copy-start.18 = (f32[32]{0:T(128)S(1)}, f32[32]{0:T(128)}, u32[]{:S(2)}) copy-start(f32[32]{0:T(128)} %get-tuple-element.873) | copy-start | bytes 388
  110.6 211.1 %copy-start.17 = (f32[32]{0:T(128)S(1)}, f32[32]{0:T(128)}, u32[]{:S(2)}) copy-start(f32[32]{0:T(128)} %get-tuple-element.872) | copy-start | bytes 388
  110.6 212.8 %copy-start.16 = (f32[32]{0:T(128)S(1)}, f32[32]{0:T(128)}, u32[]{:S(2)}) copy-start(f32[32]{0:T(128)} %get-tuple-element.871) | copy-start | bytes 388
  110.6 214.5 %copy-start.15 = (f32[32]{0:T(128)S(1)}, f32[32]{0:T(128)}, u32[]{:S(2)}) copy-start(f32[32]{0:T(128)} %get-tuple-element.870) | copy-start | bytes 388
  110.6 216.1 %copy-start.32 = (f32[32]{0:T(128)S(1)}, f32[32]{0:T(128)}, u32[]{:S(2)}) copy-start(f32[32]{0:T(128)} %get-tuple-element.869) | copy-start | bytes 388
  110.6 217.8 %copy-start.14 = (f32[32]{0:T(128)S(1)}, f32[32]{0:T(128)}, u32[]{:S(2)}) copy-start(f32[32]{0:T(128)} %get-tuple-element.868) | copy-start | bytes 388
  110.6 219.4 %copy-start.13 = (f32[32]{0:T(128)S(1)}, f32[32]{0:T(128)}, u32[]{:S(2)}) copy-start(f32[32]{0:T(128)} %get-tuple-element.867) | copy-start | bytes 388
  110.6 221.0 %copy-start.12 = (f32[32]{0:T(128)S(1)}, f32[32]{0:T(128)}, u32[]{:S(2)}) copy-start(f32[32]{0:T(128)} %get-tuple-element.866) | copy-start | bytes 388
  110.6 229.6 %copy-start.31 = (f32[32]{0:T(128)S(1)}, f32[32]{0:T(128)}, u32[]{:S(2)}) copy-start(f32[32]{0:T(128)} %get-tuple-element.861) | copy-start | bytes 388
  111.6 1.4 copy-start.3
  213.8 2.1 copy-start.9
  293.9 4.0 copy-start
where the time goes:
time: 469 us; the launch traced here: 461 us
  local copies, waits for them, and re-layouts  153 us (33%)
  matrix products  153 us (33%)
  blocking collectives  68.9 us (15%)
  other arithmetic  28.8 us (6%)
  between operations  25.7 us (5%)
  starting transfers between devices  16.9 us (4%)
  waiting for transfers between devices  14.9 us (3%)
    unnamed x79, local copies, waits for them, and re-layouts  77.9 us
    psum x1, blocking collectives, shards(): gram = lax.psum(local_gram, ('slab', 'tile'))  68.9 us
    dot_general x35, matrix products, upper_solve(): jnp.dot(factor[row_index], solved, precision=lax.Precision.HIGHEST, prefe...  48.9 us
    dot_general x1, matrix products, shards(): jnp.dot(mixing.T, columns, precision=lax.Precision.HIGHEST, preferred_ele...  48 us
    dot_general x1, matrix products, shards(): jnp.dot(columns, columns.T, precision=lax.Precision.HIGHEST, preferred_el...  28.8 us
    mul x1, local copies, waits for them, and re-layouts, shards(): scaled = basis.astype(jnp.float32) * sigma[:, None, None, None, None]  28.1 us
    dot_general x35, matrix products, upper_factor(): jnp.dot(above, factor, precision=lax.Precision.HIGHEST, preferred_element...  27.4 us
    slice x34, local copies, waits for them, and re-layouts, upper_factor(): pivot = jnp.sqrt(remainder[column_index])  20.3 us
  transfers between devices with their start and end apart: 9, of which 7 were waited for; matrix products, arithmetic and copies ran while one was open for 16% of the time, Pallas kernels for 0%

commit v1 on v0

v1 whole, which is shorter than its diff:
```python
import functools
import math

import jax
import jax.numpy as jnp
from jax import lax
from jax.experimental import pallas as pl
from jax.experimental.pallas import tpu as pltpu
from jax.sharding import PartitionSpec as P

step_size = 0.25
RANK = 32
SNAPS = 3
K = RANK + SNAPS
SUB = 8
LANES = 128
WIDE = RANK * SUB
F32 = jnp.float32
BF16 = jnp.bfloat16
HIGHEST = lax.Precision.HIGHEST


def iota(shape, dim):
    return lax.broadcasted_iota(jnp.int32, shape, dim)


def extended(block, sides, width):
    for axis, dim in sides:
        count = lax.axis_size(axis)
        forward = [(i, i + 1) for i in range(count - 1)]
        forward.append((count - 1, 0))
        backward = [(target, source) for source, target in forward]
        low = lax.ppermute(
            lax.slice_in_dim(block, block.shape[dim] - width, None, axis=dim), axis, forward
        )
        high = lax.ppermute(lax.slice_in_dim(block, 0, width, axis=dim), axis, backward)
        block = jnp.concatenate([low, block, high], axis=dim)
    return block


def advance(padded, viscosity):
    centre = padded[:, 1:-1, 1:-1, :]
    forward_x = padded[:, 2:, 1:-1, :]
    backward_x = padded[:, :-2, 1:-1, :]
    forward_z = padded[:, 1:-1, 2:, :]
    backward_z = padded[:, 1:-1, :-2, :]
    walled = jnp.pad(centre, ((0, 0), (0, 0), (0, 0), (1, 1)))
    above_y = walled[..., 2:]
    below_y = walled[..., :-2]
    laplace = forward_x + backward_x + forward_z + backward_z + above_y + below_y - 6.0 * centre
    carried = (
        centre[0:1] * (forward_x - backward_x)
        + centre[1:2] * (above_y - below_y)
        + centre[2:3] * (forward_z - backward_z)
    )
    return centre + step_size * (viscosity * laplace - 0.5 * carried)


def pieces(values, count):
    parts = []
    for _ in range(count):
        part = values.astype(BF16)
        parts.append(part)
        values = values - part.astype(F32)
    return parts


def matched(product, rows):
    same = iota(product.shape, 0) % SUB == iota(product.shape, 1) % SUB
    summed = jnp.where(same, product, 0.0).reshape(rows, SUB, WIDE).sum(1)
    pick = (iota((WIDE, LANES), 0) // SUB == iota((WIDE, LANES), 1)).astype(F32)
    return jnp.dot(summed, pick, precision=HIGHEST, preferred_element_type=F32)


def basis_columns(x_ref):
    tiles = x_ref.shape[2]
    return jnp.concatenate([x_ref[:, 0, t].reshape(WIDE, LANES) for t in range(tiles)], axis=1)


def basis_gram_kernel(x_ref, out_ref, total):
    step = pl.program_id(0)

    @pl.when(step == 0)
    def _():
        total[...] = jnp.zeros_like(total)

    columns = basis_columns(x_ref)
    total[...] += lax.dot_general(
        columns, columns, (((1,), (1,)), ((), ())), preferred_element_type=F32
    )

    @pl.when(step == pl.num_programs(0) - 1)
    def _():
        out_ref[...] = matched(total[...], RANK)


def snap_gram_kernel(s_ref, x_ref, out_ref, total, squares):
    step = pl.program_id(0)
    tiles = s_ref.shape[2]

    @pl.when(step == 0)
    def _():
        total[...] = jnp.zeros_like(total)
        squares[...] = jnp.zeros_like(squares)

    rows = []
    for s in range(SNAPS):
        flat = jnp.concatenate([s_ref[s, 0, t] for t in range(tiles)], axis=1)
        rows.extend(pieces(flat, 3))
    rows = jnp.concatenate(rows, axis=0)
    total[...] += lax.dot_general(
        rows, basis_columns(x_ref), (((1,), (1,)), ((), ())), preferred_element_type=F32
    )
    for a in range(SNAPS):
        for b in range(a + 1):
            squares[3 * a + b] += (s_ref[a, 0] * s_ref[b, 0]).sum(0)

    @pl.when(step == pl.num_programs(0) - 1)
    def _():
        by_part = matched(total[...], 3 * SNAPS)
        row = iota((SUB, LANES), 0)
        lane = iota((SUB, LANES), 1)
        result = jnp.zeros((SUB, LANES), F32)
        for s in range(SNAPS):
            line = by_part[3 * s : 3 * s + 1] + by_part[3 * s + 1 : 3 * s + 2] + by_part[3 * s + 2 : 3 * s + 3]
            result = jnp.where(row == s, line, result)
        for a in range(SNAPS):
            for b in range(a + 1):
                value = jnp.sum(squares[3 * a + b])
                result = jnp.where((row == a) & (lane == RANK + b), value, result)
        out_ref[...] = result


def mix_kernel(row_scale, gb_ref, gs_ref, sigma_ref, rotation_ref, factor_ref, weight_ref, snap_ref):
    rows = 40
    row = iota((rows, LANES), 0)
    lane = iota((rows, LANES), 1)
    low = jnp.concatenate([gb_ref[...], gs_ref[...]], axis=0)
    weight = jnp.where(iota((1, LANES), 1) < RANK, sigma_ref[...], 1.0)
    wide_weight = jnp.broadcast_to(weight, (LANES, LANES))
    low = low * weight * wide_weight.T[:rows]
    high = jnp.concatenate([low, jnp.zeros((LANES - rows, LANES), F32)], axis=0).T[:rows]
    gram = jnp.where((row < RANK) & (lane >= RANK), high, low)
    upper_right = (row >= RANK) & (lane > row)
    gram = jnp.where(upper_right, high, gram)
    gram = jnp.where((lane < K) & (row < K), gram, 0.0)
    start = gram + jnp.where((lane == row + 64) | ((lane == row) & (row >= K)), 1.0, 0.0)
    blocks = [start[SUB * b : SUB * b + SUB] for b in range(rows // SUB)]
    sub = iota((SUB, LANES), 0)
    for i in range(K):
        at, inner = divmod(i, SUB)
        pivot_row = blocks[at][inner : inner + 1, :]
        scaled = pivot_row / pivot_row[:, i : i + 1]
        for b in range(at, rows // SUB):
            column = blocks[b][:, i : i + 1]
            update = column * scaled
            if b == at:
                update = jnp.where(sub > inner, update, 0.0)
            blocks[b] = blocks[b] - update
    done = jnp.concatenate(blocks, axis=0)
    pivots = jnp.sum(jnp.where(lane == row, done, 0.0), axis=1, keepdims=True)
    done = done / jnp.sqrt(pivots)
    factor = jnp.where(lane >= row, done, 0.0) * (1.0 / row_scale)
    factor_ref[...] = factor[:K, :K]
    inverse = jnp.where(row < K, done, 0.0)
    mixed = row_scale * lax.dot_general(
        rotation_ref[...],
        inverse,
        (((0,), (0,)), ((), ())),
        precision=HIGHEST,
        preferred_element_type=F32,
    )
    mixed = mixed[:RANK]
    sigma_lane = jnp.concatenate([jnp.zeros((1, 64), F32), sigma_ref[:, :64]], axis=1)
    spread = ((iota((LANES, WIDE), 0) - 64) == iota((LANES, WIDE), 1) // SUB).astype(BF16)
    same = iota((WIDE, WIDE), 0) % SUB == iota((WIDE, WIDE), 1) % SUB
    for part, values in enumerate(pieces(mixed * sigma_lane, 2)):
        wide = jnp.dot(values, spread, preferred_element_type=F32)
        tall = jnp.broadcast_to(wide[:, None, :], (RANK, SUB, WIDE)).reshape(WIDE, WIDE)
        weight_ref[WIDE * part : WIDE * part + WIDE] = jnp.where(same, tall, 0.0).astype(BF16)
    for s in range(SNAPS):
        column = mixed[:, 64 + RANK + s : 64 + RANK + s + 1]
        snap_ref[s] = jnp.broadcast_to(column[:, :, None], (RANK, SUB, LANES))


def apply_kernel(w_ref, c_ref, s_ref, x_ref, o_ref):
    tiles = x_ref.shape[2]
    for t in range(0, tiles, 2):
        pair = jnp.concatenate(
            [x_ref[:, 0, t].reshape(WIDE, LANES), x_ref[:, 0, t + 1].reshape(WIDE, LANES)], axis=1
        )
        both = jnp.dot(w_ref[...], pair, preferred_element_type=F32)
        both = both[:WIDE] + both[WIDE:]
        for half in range(2):
            value = both[:, LANES * half : LANES * half + LANES].reshape(RANK, SUB, LANES)
            for s in range(SNAPS):
                value = value + c_ref[s] * s_ref[s, 0, t + half][None]
            o_ref[:, 0, t + half] = value.astype(BF16)


params = pltpu.CompilerParams(vmem_limit_bytes=60 << 20)


def cost(flops, moved):
    return pl.CostEstimate(flops=flops, bytes_accessed=moved, transcendentals=0)


def shards(velocity, viscosity, basis, sigma, rotation):
    current = velocity
    history = [velocity]
    for repeat in range(2):
        padded = extended(current, (("slab", 1), ("tile", 2)), 1)
        current = advance(padded, viscosity)
        history.append(current)
    snapshots = lax.all_to_all(jnp.stack(history), "tile", split_axis=2, concat_axis=3, tiled=True)
    _, parts, width, deep, lanes = basis.shape
    planes, tiles = parts * width, deep // SUB
    row_count = planes * deep * lanes * lax.axis_size("slab") * lax.axis_size("tile")
    row_scale = math.sqrt(row_count)
    modes = basis.reshape(RANK, planes, tiles, SUB, LANES)
    snaps = snapshots.reshape(SNAPS, planes, tiles, SUB, LANES)
    mode_spec = pl.BlockSpec((RANK, 1, tiles, SUB, LANES), lambda i: (0, i, 0, 0, 0))
    snap_spec = pl.BlockSpec((SNAPS, 1, tiles, SUB, LANES), lambda i: (0, i, 0, 0, 0))
    basis_gram = pl.pallas_call(
        basis_gram_kernel,
        grid=(planes,),
        in_specs=[mode_spec],
        out_specs=pl.BlockSpec((RANK, LANES), lambda i: (0, 0)),
        out_shape=jax.ShapeDtypeStruct((RANK, LANES), F32),
        scratch_shapes=[pltpu.VMEM((WIDE, WIDE), F32)],
        compiler_params=params,
        cost_estimate=cost(6_000_000_000, 12_600_000),
        name="basis_gram",
    )(modes)
    snap_gram = pl.pallas_call(
        snap_gram_kernel,
        grid=(planes,),
        in_specs=[snap_spec, mode_spec],
        out_specs=pl.BlockSpec((SUB, LANES), lambda i: (0, 0)),
        out_shape=jax.ShapeDtypeStruct((SUB, LANES), F32),
        scratch_shapes=[
            pltpu.VMEM((3 * SNAPS * SUB, WIDE), F32),
            pltpu.VMEM((9, SUB, LANES), F32),
        ],
        compiler_params=params,
        cost_estimate=cost(6_000_000_000, 15_000_000),
        name="snap_gram",
    )(snaps, modes)
    whole = lax.psum(jnp.concatenate([basis_gram, snap_gram], axis=0), ("slab", "tile"))
    sigma_row = jnp.pad(sigma[None], ((0, 0), (0, LANES - RANK)))
    rotation_wide = jnp.pad(rotation, ((0, 40 - K), (0, LANES - RANK)))
    factor, weight, snap_weight = pl.pallas_call(
        functools.partial(mix_kernel, row_scale),
        out_shape=(
            jax.ShapeDtypeStruct((K, K), F32),
            jax.ShapeDtypeStruct((2 * WIDE, WIDE), BF16),
            jax.ShapeDtypeStruct((SNAPS, RANK, SUB, LANES), F32),
        ),
        compiler_params=params,
        name="mix",
    )(whole[:RANK], whole[RANK:], sigma_row, rotation_wide)
    rotated = pl.pallas_call(
        apply_kernel,
        grid=(planes,),
        in_specs=[
            pl.BlockSpec((2 * WIDE, WIDE), lambda i: (0, 0)),
            pl.BlockSpec((SNAPS, RANK, SUB, LANES), lambda i: (0, 0, 0, 0)),
            snap_spec,
            mode_spec,
        ],
        out_specs=mode_spec,
        out_shape=jax.ShapeDtypeStruct(modes.shape, BF16),
        compiler_params=params,
        cost_estimate=cost(12_000_000_000, 27_000_000),
        name="apply",
    )(weight, snap_weight, snaps, modes)
    return (current, factor, rotated.reshape(basis.shape))


def solution(mesh):
    in_specs = (
        P(None, "slab", "tile", None),
        P("slab", "tile", None),
        P(None, None, ("slab", "tile"), None, None),
        P(),
        P(),
    )
    out_specs = (P(None, "slab", "tile", None), P(), P(None, None, ("slab", "tile"), None, None))
    return jax.shard_map(shards, mesh=mesh, in_specs=in_specs, out_specs=out_specs, check_vma=False)
```

time: 469 us -> 174 us (0.37); the launches traced: 461 us -> 173 us
  matrix products: 153 us -> 0 us
  local copies, waits for them, and re-layouts: 153 us -> 7.6 us
  Pallas kernels: 0 us -> 47.3 us
  between operations: 25.7 us -> 0.77 us
  other arithmetic: 28.8 us -> 5.9 us
  waiting for transfers between devices: 14.9 us -> 29.7 us
    dot_general x72 -> x0, matrix products: 153 us -> none  [the longest x35 48.9 us: upper_solve(): jnp.dot(factor[row_index], solved, precision=lax.Precision.HIGHEST, prefe...]
    unnamed x79 -> x24, local copies, waits for them, and re-layouts: 77.9 us -> 1.13 us
    pallas_call x0 -> x4, Pallas kernels: none -> 47.3 us  [the longest x1 17.7 us: shards(): pl.pallas_call(apply_kernel, grid=(planes,), in_specs=[pl.BlockSpec((2 *...]
    slice x73 -> x2, local copies, waits for them, and re-layouts: 30.5 us -> 1.2 us  [the longest x1 0.61 us: shards(): whole[:RANK]]
    mul x1 -> x0, local copies, waits for them, and re-layouts: 28.1 us -> none  [shards(): scaled = basis.astype(jnp.float32) * sigma[:, None, None, None, None]]
    all_to_all x1, waiting for transfers between devices: 0.01 us -> 12.7 us  [shards(): lax.all_to_all(jnp.stack(history), 'tile', split_axis=2, concat_axis=3, t...]
    mul x1 -> x0, other arithmetic: 11.8 us -> none  [shards(): scaled = basis.astype(jnp.float32) * sigma[:, None, None, None, None]]
    concatenate x1, other arithmetic: 10.1 us -> 0.69 us  [shards(): jnp.concatenate([basis_gram, snap_gram], axis=0)]
  transfers between devices with their start and end apart: 9 -> 9, of which waited for: 7 -> 9; matrix products, arithmetic and copies ran while one was open for 16% -> 3% of each run, Pallas kernels for 0% -> 7%
where the time goes in v1:
time: 174 us; the launch traced here: 173 us
  blocking collectives  64.7 us (37%)
  Pallas kernels  47.3 us (27%)
  waiting for transfers between devices  29.7 us (17%)
  starting transfers between devices  17 us (10%)
  local copies, waits for them, and re-layouts  7.6 us (4%)
  other arithmetic  5.9 us (3%)
    psum x1, blocking collectives, shards(): lax.psum(jnp.concatenate([basis_gram, snap_gram], axis=0), ('slab', 'tile'))  64.7 us
    pallas_call x1, Pallas kernels, shards(): pl.pallas_call(apply_kernel, grid=(planes,), in_specs=[pl.BlockSpec((2 *...  17.7 us
    all_to_all x1, waiting for transfers between devices, shards(): lax.all_to_all(jnp.stack(history), 'tile', split_axis=2, concat_axis=3, t...  12.7 us
    pallas_call x1, Pallas kernels, shards(): pl.pallas_call(snap_gram_kernel, grid=(planes,), in_specs=[snap_spec, mod...  12.4 us
    pallas_call x1, Pallas kernels, shards(): pl.pallas_call(basis_gram_kernel, grid=(planes,), in_specs=[mode_spec], o...  12.1 us
    ppermute x4, starting transfers between devices, extended(): lax.ppermute(lax.slice_in_dim(block, block.shape[dim] - width, None, axis...  9.18 us
    ppermute x4, waiting for transfers between devices, extended(): lax.ppermute(lax.slice_in_dim(block, 0, width, axis=dim), axis, backward)  9.1 us
    ppermute x4, waiting for transfers between devices, extended(): lax.ppermute(lax.slice_in_dim(block, block.shape[dim] - width, None, axis...  7.96 us
  transfers between devices with their start and end apart: 9, of which 9 were waited for; matrix products, arithmetic and copies ran while one was open for 3% of the time, Pallas kernels for 7%

profile of v1, /device:TPU:1, one launch (start us, length us, event | category | flops | bytes accessed | tf_op | source)
XLA Modules:
  0.0 173.0 jit_solution(5517012599141504785)
XLA Ops:
  0.6 0.0 copy-start
  0.6 0.8 fusion.2
  1.5 4.3 %collective-permute-start.1 = (f32[3,1,16,128]{3,2,0,1:T(8,128)S(1)}, f32[3,1,16,128]{3,2,0,1:T(8,128)S(1)}, u32[]{:S(2)}, u32[]{:S(2)}) collective-permute-start(f32[3,1,16,128]{3,2,0,1:T(8,128)S(1)} %get-tuple-element.27), channel_id=1, source_target_pairs={{0,8},{8,16},{16,24},{24,32},{32,40},{40,48},{48,56},{56,64},{64,7... | collective-permute-start | bytes 73736 | tf_op jit(solution)/shard_map/ppermute | solution.py:33
  5.8 0.0 collective-permute-start
  5.8 0.9 collective-permute-done.1
  6.7 0.0 copy-start.5
  6.7 1.3 copy_bitcast_fusion
  8.0 2.5 %collective-permute-done = f32[3,1,16,128]{3,2,0,1:T(8,128)S(1)} collective-permute-done((f32[3,1,16,128]{3,2,0,1:T(8,128)S(1)}, f32[3,1,16,128]{3,2,0,1:T(8,128)S(1)}, u32[]{:S(2)}, u32[]{:S(2)}) %collective-permute-start) | collective-permute-done | bytes 24608 | tf_op jit(solution)/shard_map/ppermute | solution.py:36
  10.5 0.1 fusion
  10.6 3.9 %collective-permute-start.2 = (f32[3,34,1,128]{3,2,0,1:T(1,128)S(1)}, f32[3,34,1,128]{3,2,0,1:T(1,128)S(1)}, u32[]{:S(2)}, u32[]{:S(2)}) collective-permute-start(f32[3,34,1,128]{3,2,0,1:T(1,128)S(1)} %get-tuple-element.14), channel_id=1, source_target_pairs={{1,0},{2,1},{3,2},{4,3},{5,4},{6,5},{7,6},{0,7},{9,8},{10,9},{11,1... | collective-permute-start | bytes 156680 | tf_op jit(solution)/shard_map/ppermute | solution.py:36
  14.6 0.0 collective-permute-start.3
  14.6 0.0 copy-done
  14.6 0.1 slice_bitcast_fusion.5
  14.6 0.1 copy.17
  14.7 1.1 collective-permute-done.2
  15.8 3.9 %collective-permute-done.3 = f32[3,34,1,128]{3,2,0,1:T(1,128)S(1)} collective-permute-done((f32[3,34,1,128]{3,2,0,1:T(1,128)S(1)}, f32[3,34,1,128]{3,2,0,1:T(1,128)S(1)}, u32[]{:S(2)}, u32[]{:S(2)}) %collective-permute-start.3) | collective-permute-done | bytes 52256 | tf_op jit(solution)/shard_map/ppermute | solution.py:33
  19.6 0.0 copy-done.5
  19.6 0.9 multiply_add_fusion.1
  20.5 3.4 %collective-permute-start.5 = (f32[3,1,16,128]{3,2,0,1:T(8,128)S(1)}, f32[3,1,16,128]{3,2,0,1:T(8,128)S(1)}, u32[]{:S(2)}, u32[]{:S(2)}) collective-permute-start(f32[3,1,16,128]{3,2,0,1:T(8,128)S(1)} %get-tuple-element.21), channel_id=1, source_target_pairs={{0,8},{8,16},{16,24},{24,32},{32,40},{40,48},{48,56},{56,64},{64,7... | collective-permute-start | bytes 73736 | tf_op jit(solution)/shard_map/ppermute | solution.py:33
  23.9 0.0 collective-permute-start.4
  23.9 0.9 collective-permute-done.5
  24.9 4.1 %collective-permute-done.4 = f32[3,1,16,128]{3,2,0,1:T(8,128)S(1)} collective-permute-done((f32[3,1,16,128]{3,2,0,1:T(8,128)S(1)}, f32[3,1,16,128]{3,2,0,1:T(8,128)S(1)}, u32[]{:S(2)}, u32[]{:S(2)}) %collective-permute-start.4) | collective-permute-done | bytes 24608 | tf_op jit(solution)/shard_map/ppermute | solution.py:36
  29.0 0.1 pad_maximum_fusion.15
  29.1 0.1 collective-permute-start.6
  29.2 1.5 collective-permute-start.7
  30.6 0.1 slice_bitcast_fusion.2
  30.7 0.0 copy-start.1
  30.7 0.0 copy-start.3
  30.7 1.4 collective-permute-done.6
  32.1 2.2 %collective-permute-done.7 = f32[3,34,1,128]{3,2,0,1:T(1,128)S(1)} collective-permute-done((f32[3,34,1,128]{3,2,0,1:T(1,128)S(1)}, f32[3,34,1,128]{3,2,0,1:T(1,128)S(1)}, u32[]{:S(2)}, u32[]{:S(2)}) %collective-permute-start.7) | collective-permute-done | bytes 52256 | tf_op jit(solution)/shard_map/ppermute | solution.py:33
  34.3 0.0 copy-start.6
  34.3 0.9 fusion.3
  35.2 1.6 pad_maximum_fusion
  36.8 0.0 copy-done.1
  36.8 0.0 copy-done.3
  36.8 0.0 copy-start.7
  36.8 0.0 copy-start.9
  36.8 0.0 copy-done.6
  36.8 3.8 %all-to-all-start = ((f32[3,3,32,16,128]{4,3,1,0,2:T(8,128)}), f32[3,3,32,16,128]{4,3,1,0,2:T(8,128)S(1)}, u32[]{:S(2)}, u32[]{:S(2)}) async-start(f32[3,3,32,16,128]{4,3,1,0,2:T(8,128)} %pad_maximum_fusion), calls=%async_computation | async-start | bytes 4718592 | tf_op jit(solution)/shard_map/all_to_all | solution.py:215
  40.6 0.0 copy-done.7
  40.6 0.1 copy.21
  40.7 0.0 copy-done.9
  40.7 0.6 pad.17.sigma_ref
  41.3 0.6 pad.18.rotation_ref
  41.9 0.0 copy-start.2
  41.9 0.0 copy-start.4
  41.9 12.1 %basis_gram.1 = f32[32,128]{1,0:T(8,128)} custom-call(bf16[32,12,16,8,128]{4,3,2,1,0:T(8,128)(2,1)} %bitcast.30), custom_call_target="tpu_custom_call" | custom-call | flops 6000000000 | bytes 12600000 | tf_op jit(solution)/shard_map/basis_gram/pallas_call | solution.py:224
  54.0 0.0 copy-done.2
  54.0 0.0 copy-done.4
  54.0 1.8 %multiply_add_fusion = f32[3,32,16,128]{3,2,0,1:T(8,128)S(1)} fusion(f32[3,32,16,128]{3,2,0,1:T(8,128)S(1)} %multiply_add_fusion.1, f32[3,1,16,128]{3,2,0,1:T(8,128)S(1)} %collective-permute-done.4, f32[3,1,16,128]{3,2,0,1:T(8,128)S(1)} %collective-permute-done.5, f32[3,34,1,128]{3,2,0,1:T(1,128)} %copy-done.6, ...), kind=kLoop, calls=%fused_computation.17 | loop fusion | flops 5505024 | bytes 2775040 | tf_op jit(solution)/shard_map/add | solution.py:56
  55.8 0.9 copy.22
  56.8 12.7 %all-to-all-done = f32[3,3,32,16,128]{4,3,1,0,2:T(8,128)S(1)} async-done(((f32[3,3,32,16,128]{4,3,1,0,2:T(8,128)}), f32[3,3,32,16,128]{4,3,1,0,2:T(8,128)S(1)}, u32[]{:S(2)}, u32[]{:S(2)}) %all-to-all-start) | async-done | bytes 2359328 | tf_op jit(solution)/shard_map/all_to_all | solution.py:215
  69.4 1.8 %copy.20 = f32[3,3,8,4,16,128]{5,4,2,3,1,0:T(8,128)} copy(f32[3,3,8,4,16,128]{5,4,1,0,3,2:T(8,128)S(1)} %bitcast.27) | data formatting | bytes 4718592 | tf_op jit(solution)/shard_map/all_to_all | solution.py:215
  71.2 0.0 copy-start.8
  71.2 12.4 %snap_gram.1 = f32[8,128]{1,0:T(8,128)} custom-call(f32[3,12,16,8,128]{4,3,2,1,0:T(8,128)} %bitcast.28, bf16[32,12,16,8,128]{4,3,2,1,0:T(8,128)(2,1)} %bitcast.31), custom_call_target="tpu_custom_call" | custom-call | flops 6000000000 | bytes 15000000 | tf_op jit(solution)/shard_map/snap_gram/pallas_call | solution.py:235
  83.6 0.0 copy-done.8
  83.6 0.7 pad_maximum_fusion.16
  84.3 64.7 %psum.7 = f32[40,128]{1,0:T(8,128)S(1)} all-reduce(f32[40,128]{1,0:T(8,128)S(1)} %pad_maximum_fusion.16), channel_id=1, replica_groups=mesh['slab'=16,'tile'=8] {'slab','tile'}, use_global_device_ids=true, to_apply=%region_0.1 | all-reduce | flops 5120 | bytes 40960 | tf_op jit(solution)/shard_map/psum | solution.py:249
  149.0 0.6 slice.130.gs_ref
  149.6 0.6 slice.129.gb_ref
  150.2 5.1 %mix.1 = (f32[35,35]{1,0:T(8,128)}, bf16[512,256]{1,0:T(8,128)(2,1)}, f32[3,32,8,128]{3,2,1,0:T(8,128)}) custom-call(f32[32,128]{1,0:T(8,128)} %slice.129.gb_ref, f32[8,128]{1,0:T(8,128)} %slice.130.gs_ref, f32[1,128]{1,0:T(1,128)} %pad.17.sigma_ref, f32[40,128]{1,0:T(8,128)} %pad.18.rotation_ref), custom_call_target="tpu_custom_call" | custom-call | tf_op jit(solution)/shard_map/mix/pallas_call | solution.py:252
  155.3 17.7 %apply.1 = bf16[32,12,16,8,128]{4,3,2,1,0:T(8,128)(2,1)} custom-call(bf16[512,256]{1,0:T(8,128)(2,1)} %get-tuple-element.7.w_ref, f32[3,32,8,128]{3,2,1,0:T(8,128)} %get-tuple-element.8.c_ref, f32[3,12,16,8,128]{4,3,2,1,0:T(8,128)} %bitcast.29, bf16[32,12,16,8,128]{4,3,2,1,0:T(8,128)(2,1)} %bitcast.32), custom_call_target="tpu_custom_call" | custom-call | flops 12000000000 | bytes 27000000 | tf_op jit(solution)/shard_map/apply/pallas_call | solution.py:262
  (3 shorter events, 0.0 us)
Async XLA Ops:
  0.6 13.9 %copy-start = (f32[3,32,16,128]{3,2,1,0:T(8,128)S(1)}, f32[3,32,16,128]{3,2,1,0:T(8,128)}, u32[]{:S(2)}) copy-start(f32[3,32,16,128]{3,2,1,0:T(8,128)} %param.5) | copy-start | bytes 2359300
  1.5 5.3 %collective-permute-start.1 = (f32[3,1,16,128]{3,2,0,1:T(8,128)S(1)}, f32[3,1,16,128]{3,2,0,1:T(8,128)S(1)}, u32[]{:S(2)}, u32[]{:S(2)}) collective-permute-start(f32[3,1,16,128]{3,2,0,1:T(8,128)S(1)} %get-tuple-element.27), channel_id=1, source_target_pairs={{0,8},{8,16},{16,24},{24,32},{32,40},{40,48},{48,56},{56,64},{64,7... | collective-permute-start | bytes 73736 | tf_op jit(solution)/shard_map/ppermute | solution.py:33
  5.8 4.8 %collective-permute-start = (f32[3,1,16,128]{3,2,0,1:T(8,128)S(1)}, f32[3,1,16,128]{3,2,0,1:T(8,128)S(1)}, u32[]{:S(2)}, u32[]{:S(2)}) collective-permute-start(f32[3,1,16,128]{3,2,0,1:T(8,128)S(1)} %get-tuple-element.26), channel_id=1, source_target_pairs={{8,0},{16,8},{24,16},{32,24},{40,32},{48,40},{56,48},{64,56},{72,6... | collective-permute-start | bytes 73736 | tf_op jit(solution)/shard_map/ppermute | solution.py:36
  6.7 12.9 %copy-start.5 = (f32[32,16,128]{2,1,0:T(8,128)S(1)}, f32[32,16,128]{2,1,0:T(8,128)}, u32[]{:S(2)}) copy-start(f32[32,16,128]{2,1,0:T(8,128)} %param.6) | copy-start | bytes 786436
  10.6 5.1 %collective-permute-start.2 = (f32[3,34,1,128]{3,2,0,1:T(1,128)S(1)}, f32[3,34,1,128]{3,2,0,1:T(1,128)S(1)}, u32[]{:S(2)}, u32[]{:S(2)}) collective-permute-start(f32[3,34,1,128]{3,2,0,1:T(1,128)S(1)} %get-tuple-element.14), channel_id=1, source_target_pairs={{1,0},{2,1},{3,2},{4,3},{5,4},{6,5},{7,6},{0,7},{9,8},{10,9},{11,1... | collective-permute-start | bytes 156680 | tf_op jit(solution)/shard_map/ppermute | solution.py:36
  14.6 5.1 %collective-permute-start.3 = (f32[3,34,1,128]{3,2,0,1:T(1,128)S(1)}, f32[3,34,1,128]{3,2,0,1:T(1,128)S(1)}, u32[]{:S(2)}, u32[]{:S(2)}) collective-permute-start(f32[3,34,1,128]{3,2,0,1:T(1,128)S(1)} %get-tuple-element.15), channel_id=1, source_target_pairs={{0,1},{1,2},{2,3},{3,4},{4,5},{5,6},{6,7},{7,0},{8,9},{9,10},{10,1... | collective-permute-start | bytes 156680 | tf_op jit(solution)/shard_map/ppermute | solution.py:33
  20.5 4.4 %collective-permute-start.5 = (f32[3,1,16,128]{3,2,0,1:T(8,128)S(1)}, f32[3,1,16,128]{3,2,0,1:T(8,128)S(1)}, u32[]{:S(2)}, u32[]{:S(2)}) collective-permute-start(f32[3,1,16,128]{3,2,0,1:T(8,128)S(1)} %get-tuple-element.21), channel_id=1, source_target_pairs={{0,8},{8,16},{16,24},{24,32},{32,40},{40,48},{48,56},{56,64},{64,7... | collective-permute-start | bytes 73736 | tf_op jit(solution)/shard_map/ppermute | solution.py:33
  23.9 5.1 %collective-permute-start.4 = (f32[3,1,16,128]{3,2,0,1:T(8,128)S(1)}, f32[3,1,16,128]{3,2,0,1:T(8,128)S(1)}, u32[]{:S(2)}, u32[]{:S(2)}) collective-permute-start(f32[3,1,16,128]{3,2,0,1:T(8,128)S(1)} %get-tuple-element.22), channel_id=1, source_target_pairs={{8,0},{16,8},{24,16},{32,24},{40,32},{48,40},{56,48},{64,56},{72,6... | collective-permute-start | bytes 73736 | tf_op jit(solution)/shard_map/ppermute | solution.py:36
  29.1 3.0 %collective-permute-start.6 = (f32[3,34,1,128]{3,2,0,1:T(1,128)S(1)}, f32[3,34,1,128]{3,2,0,1:T(1,128)S(1)}, u32[]{:S(2)}, u32[]{:S(2)}) collective-permute-start(f32[3,34,1,128]{3,2,0,1:T(1,128)S(1)} %get-tuple-element.12), channel_id=1, source_target_pairs={{1,0},{2,1},{3,2},{4,3},{5,4},{6,5},{7,6},{0,7},{9,8},{10,9},{11,1... | collective-permute-start | bytes 156680 | tf_op jit(solution)/shard_map/ppermute | solution.py:36
  29.2 5.2 %collective-permute-start.7 = (f32[3,34,1,128]{3,2,0,1:T(1,128)S(1)}, f32[3,34,1,128]{3,2,0,1:T(1,128)S(1)}, u32[]{:S(2)}, u32[]{:S(2)}) collective-permute-start(f32[3,34,1,128]{3,2,0,1:T(1,128)S(1)} %get-tuple-element.13), channel_id=1, source_target_pairs={{0,1},{1,2},{2,3},{3,4},{4,5},{5,6},{6,7},{7,0},{8,9},{9,10},{10,1... | collective-permute-start | bytes 156680 | tf_op jit(solution)/shard_map/ppermute | solution.py:33
  30.7 6.1 %copy-start.1 = (f32[32,16,128]{2,1,0:T(8,128)}, f32[32,16,128]{2,1,0:T(8,128)S(1)}, u32[]{:S(2)}) copy-start(f32[32,16,128]{2,1,0:T(8,128)S(1)} %get-tuple-element.19) | copy-start | bytes 786436
  30.7 6.1 %copy-start.3 = (f32[32,16,128]{2,1,0:T(8,128)}, f32[32,16,128]{2,1,0:T(8,128)S(1)}, u32[]{:S(2)}) copy-start(f32[32,16,128]{2,1,0:T(8,128)S(1)} %get-tuple-element.20) | copy-start | bytes 786436
  34.3 2.5 %copy-start.6 = (f32[3,34,1,128]{3,2,0,1:T(1,128)}, f32[3,34,1,128]{3,2,0,1:T(1,128)S(1)}, u32[]{:S(2)}) copy-start(f32[3,34,1,128]{3,2,0,1:T(1,128)S(1)} %collective-permute-done.7) | copy-start | bytes 156676
  36.8 3.8 %copy-start.7 = (f32[35,32]{0,1:T(8,128)S(1)}, f32[35,32]{0,1:T(8,128)}, u32[]{:S(2)}) copy-start(f32[35,32]{0,1:T(8,128)} %param.9) | copy-start | bytes 13444
  36.8 3.9 %copy-start.9 = (f32[32]{0:T(128)S(1)}, f32[32]{0:T(128)}, u32[]{:S(2)}) copy-start(f32[32]{0:T(128)} %param.8) | copy-start | bytes 388
  36.8 32.6 %all-to-all-start = ((f32[3,3,32,16,128]{4,3,1,0,2:T(8,128)}), f32[3,3,32,16,128]{4,3,1,0,2:T(8,128)S(1)}, u32[]{:S(2)}, u32[]{:S(2)}) async-start(f32[3,3,32,16,128]{4,3,1,0,2:T(8,128)} %pad_maximum_fusion), calls=%async_computation | async-start | bytes 4718592 | tf_op jit(solution)/shard_map/all_to_all | solution.py:215
  41.9 12.1 %copy-start.2 = (f32[32,16,128]{2,1,0:T(8,128)S(1)}, f32[32,16,128]{2,1,0:T(8,128)}, u32[]{:S(2)}) copy-start(f32[32,16,128]{2,1,0:T(8,128)} %copy-done.1) | copy-start | bytes 786436
  41.9 12.1 %copy-start.4 = (f32[32,16,128]{2,1,0:T(8,128)S(1)}, f32[32,16,128]{2,1,0:T(8,128)}, u32[]{:S(2)}) copy-start(f32[32,16,128]{2,1,0:T(8,128)} %copy-done.3) | copy-start | bytes 786436
  71.2 12.4 %copy-start.8 = (f32[32,128]{1,0:T(8,128)S(1)}, f32[32,128]{1,0:T(8,128)}, u32[]{:S(2)}) copy-start(f32[32,128]{1,0:T(8,128)} %basis_gram.1) | copy-start | bytes 49156

commit v2 on v1

v2 whole, which is shorter than its diff:
```python
import functools
import math

import jax
import jax.numpy as jnp
from jax import lax
from jax.experimental import pallas as pl
from jax.experimental.pallas import tpu as pltpu
from jax.sharding import PartitionSpec as P

step_size = 0.25
RANK = 32
SNAPS = 3
K = RANK + SNAPS
SUB = 8
LANES = 128
WIDE = RANK * SUB
F32 = jnp.float32
BF16 = jnp.bfloat16
HIGHEST = lax.Precision.HIGHEST
MESH = pl.DeviceIdType.MESH
GRAM_ROWS = 40
EXCHANGE_VMEM = 63_700_000
ROTATE_VMEM = 50 << 20


def iota(shape, dim):
    return lax.broadcasted_iota(jnp.int32, shape, dim)


def pieces(values, count):
    parts = []
    for _ in range(count):
        part = values.astype(BF16)
        parts.append(part)
        values = values - part.astype(F32)
    return parts


def matched(product, rows):
    same = iota(product.shape, 0) % SUB == iota(product.shape, 1) % SUB
    summed = jnp.where(same, product, 0.0).reshape(rows, SUB, WIDE).sum(1)
    pick = (iota((WIDE, LANES), 0) // SUB == iota((WIDE, LANES), 1)).astype(F32)
    return jnp.dot(summed, pick, precision=HIGHEST, preferred_element_type=F32)


def wide_pair(ref, *index):
    *front, tile = index
    left = ref[(slice(None), *front, tile)].reshape(WIDE, LANES)
    right = ref[(slice(None), *front, tile + 1)].reshape(WIDE, LANES)
    return jnp.concatenate([left, right], axis=1)


def advance_planes(padded, low, high, viscosity, store):
    count = viscosity.shape[0]
    depth = 2 * SUB
    row = iota((depth, LANES), 0)
    lane = iota((depth, LANES), 1)

    def plane(x, carry):
        def at(c, p):
            return padded[c, p].reshape(depth, LANES)

        flow = [at(c, x + 1) for c in range(3)]
        nu = viscosity[x].reshape(depth, LANES)
        for c in range(3):
            centre = flow[c]
            forward_x, backward_x = at(c, x + 2), at(c, x)
            forward_z = jnp.where(row == depth - 1, high[c, pl.ds(x, 1)], pltpu.roll(centre, depth - 1, 0))
            backward_z = jnp.where(row == 0, low[c, pl.ds(x, 1)], pltpu.roll(centre, 1, 0))
            above_y = jnp.where(lane == LANES - 1, 0.0, pltpu.roll(centre, LANES - 1, 1))
            below_y = jnp.where(lane == 0, 0.0, pltpu.roll(centre, 1, 1))
            laplace = forward_x + backward_x + forward_z + backward_z + above_y + below_y - 6.0 * centre
            carried = (
                flow[0] * (forward_x - backward_x)
                + flow[1] * (above_y - below_y)
                + flow[2] * (forward_z - backward_z)
            )
            store(c, x, centre + step_size * (nu * laplace - 0.5 * carried))
        return carry

    lax.fori_loop(0, count, plane, 0)


def exchange_kernel(
    slabs,
    tiles,
    vel_hbm,
    nu_hbm,
    modes_hbm,
    advanced,
    gram_ref,
    snaps,
    modes,
    flow,
    nu,
    low,
    high,
    low_edge,
    high_edge,
    products,
    squares,
    sums_one,
    sums_two,
    late_sums_one,
    late_sums_two,
    load_sem,
    mode_sem,
    own_sem,
    face_send,
    face_recv,
    bulk_send,
    bulk_recv,
    one_send,
    one_recv,
    two_send,
    two_recv,
):
    slab, tile = lax.axis_index("slab"), lax.axis_index("tile")
    planes = modes.shape[1]
    width = snaps.shape[2]
    count = nu.shape[0]

    def shifted(index, by, size):
        return lax.rem(index + by + size, size)

    loads = [
        pltpu.make_async_copy(vel_hbm, flow.at[0, :, 1 : count + 1], load_sem.at[0]),
        pltpu.make_async_copy(nu_hbm, nu, load_sem.at[1]),
    ]
    for copy in loads:
        copy.start()

    barrier = pltpu.get_barrier_semaphore()
    for d in range(1, tiles):
        pl.semaphore_signal(barrier, inc=1, device_id={"tile": shifted(tile, d, tiles)}, device_id_type=MESH)
    for d in range(1, slabs):
        pl.semaphore_signal(barrier, inc=1, device_id={"slab": shifted(slab, d, slabs)}, device_id_type=MESH)

    def mode_copy(plane):
        return pltpu.make_async_copy(modes_hbm.at[:, plane], modes.at[:, plane], mode_sem.at[plane])

    for copy in loads:
        copy.wait()
    for plane in range(planes):
        mode_copy(plane).start()

    def edges(x, carry):
        for c in range(3):
            low_edge[0, c, pl.ds(x, 1)] = flow[0, c, x + 1, 0, 0:1]
            high_edge[0, c, pl.ds(x, 1)] = flow[0, c, x + 1, 1, SUB - 1 : SUB]
        return carry

    lax.fori_loop(0, count, edges, 0)
    pl.semaphore_wait(barrier, tiles + slabs - 2)

    def faces(step):
        up_x, down_x = {"slab": shifted(slab, 1, slabs)}, {"slab": shifted(slab, -1, slabs)}
        up_z, down_z = {"tile": shifted(tile, 1, tiles)}, {"tile": shifted(tile, -1, tiles)}
        moves = [
            (low_edge.at[step], high.at[step], down_z),
            (high_edge.at[step], low.at[step], up_z),
            (flow.at[step, :, count], flow.at[step, :, 0], up_x),
            (flow.at[step, :, 1], flow.at[step, :, count + 1], down_x),
        ]
        return [
            pltpu.make_async_remote_copy(
                src_ref=source,
                dst_ref=target,
                send_sem=face_send.at[step, i],
                recv_sem=face_recv.at[step, i],
                device_id=device,
                device_id_type=MESH,
            )
            for i, (source, target, device) in enumerate(moves)
        ]

    def strip(k, owner):
        start = owner * width
        if k == 2:
            return advanced.at[:, pl.ds(start, width)]
        return flow.at[k, :, pl.ds(start + 1, width)]

    def bulk(k, d):
        owner = shifted(tile, d, tiles)
        return pltpu.make_async_remote_copy(
            src_ref=strip(k, owner),
            dst_ref=snaps.at[k, :, :, pl.ds(2 * tile, 2)],
            send_sem=bulk_send.at[k, d],
            recv_sem=bulk_recv.at[k, d],
            device_id={"tile": owner},
            device_id_type=MESH,
        )

    def own(k):
        return pltpu.make_async_copy(strip(k, tile), snaps.at[k, :, :, pl.ds(2 * tile, 2)], own_sem.at[k])

    def send_strips(k):
        for d in range(1, tiles):
            bulk(k, d).start()
        own(k).start()

    def gram_planes(first, last):
        def plane_step(plane, carry):
            mode_copy(plane).wait()
            columns = jnp.concatenate(
                [wide_pair(modes, plane, t) for t in range(0, modes.shape[2], 2)], axis=1
            )
            products[...] += lax.dot_general(
                columns, columns, (((1,), (1,)), ((), ())), preferred_element_type=F32
            )
            return carry

        lax.fori_loop(first, last, plane_step, 0)

    first_faces = faces(0)
    for copy in first_faces:
        copy.start()
    send_strips(0)
    products[...] = jnp.zeros_like(products)
    squares[...] = jnp.zeros_like(squares)
    gram_planes(0, planes // 2)
    for copy in first_faces:
        copy.wait()

    def store_first(c, x, value):
        flow[1, c, x + 1] = value.reshape(2, SUB, LANES)
        low_edge[1, c, pl.ds(x, 1)] = value[0:1]
        high_edge[1, c, pl.ds(x, 1)] = value[2 * SUB - 1 :]

    advance_planes(flow.at[0], low.at[0], high.at[0], nu, store_first)
    second_faces = faces(1)
    for copy in second_faces:
        copy.start()
    send_strips(1)
    gram_planes(planes // 2, planes)
    for copy in second_faces:
        copy.wait()

    def store_second(c, x, value):
        advanced[c, x] = value.reshape(2, SUB, LANES)

    advance_planes(flow.at[1], low.at[1], high.at[1], nu, store_second)
    send_strips(2)

    def reduce_start(axis, size, sums, send, recv):
        me = lax.axis_index(axis)
        return [
            pltpu.make_async_remote_copy(
                src_ref=sums.at[0],
                dst_ref=sums.at[1 + me],
                send_sem=send.at[d],
                recv_sem=recv.at[d],
                device_id={axis: shifted(me, d, size)},
                device_id_type=MESH,
            )
            for d in range(1, size)
        ]

    def reduce_end(axis, size, sums, copies):
        me = lax.axis_index(axis)
        sums[1 + me] = sums[0]
        for copy in copies:
            copy.wait()
        total = sums[1]
        for i in range(1, size):
            total = total + sums[1 + i]
        return total

    sums_one[0] = matched(products[...], RANK)
    basis_one = reduce_start("tile", tiles, sums_one, one_send.at[0], one_recv.at[0])
    for copy in basis_one:
        copy.start()

    snap_rows = 3 * SNAPS * SUB
    products[:snap_rows] = jnp.zeros((snap_rows, WIDE), F32)

    def piece(d, carry):
        @pl.when(d == 0)
        def _():
            for k in range(SNAPS):
                own(k).wait()

        @pl.when(d > 0)
        def _():
            for k in range(SNAPS):
                bulk(k, d).wait_recv()

        at = 2 * shifted(tile, -d, tiles)
        columns = jnp.concatenate([wide_pair(modes, p, at) for p in range(planes)], axis=1)
        rows = []
        for k in range(SNAPS):
            flat = jnp.concatenate(
                [
                    snaps[k, p // width, p % width, at + h]
                    for p in range(planes)
                    for h in range(2)
                ],
                axis=1,
            )
            rows.extend(pieces(flat, 3))
        products[:snap_rows] += lax.dot_general(
            jnp.concatenate(rows, axis=0),
            columns,
            (((1,), (1,)), ((), ())),
            preferred_element_type=F32,
        )
        for a in range(SNAPS):
            for b in range(a + 1):
                total = jnp.zeros((SUB, LANES), F32)
                for p in range(planes):
                    for h in range(2):
                        c, w = divmod(p, width)
                        total = total + snaps[a, c, w, at + h] * snaps[b, c, w, at + h]
                squares[3 * a + b] += total
        return carry

    lax.fori_loop(0, tiles // 2, piece, 0)
    sums_two[0] = reduce_end("tile", tiles, sums_one, basis_one)
    basis_two = reduce_start("slab", slabs, sums_two, two_send.at[0], two_recv.at[0])
    for copy in basis_two:
        copy.start()
    lax.fori_loop(tiles // 2, tiles, piece, 0)
    gram_ref[:RANK] = reduce_end("slab", slabs, sums_two, basis_two)
    by_part = matched(products[:snap_rows], 3 * SNAPS)
    lines = [
        by_part[3 * s : 3 * s + 1] + by_part[3 * s + 1 : 3 * s + 2] + by_part[3 * s + 2 : 3 * s + 3]
        for s in range(SNAPS)
    ]

    row = iota((SUB, LANES), 0)
    lane = iota((SUB, LANES), 1)
    result = jnp.zeros((SUB, LANES), F32)
    for s in range(SNAPS):
        result = jnp.where(row == s, lines[s], result)
    for a in range(SNAPS):
        for b in range(a + 1):
            result = jnp.where((row == a) & (lane == RANK + b), jnp.sum(squares[3 * a + b]), result)
    late_sums_one[0] = result
    late = reduce_start("tile", tiles, late_sums_one, one_send.at[1], one_recv.at[1])
    for copy in late:
        copy.start()
    late_sums_two[0] = reduce_end("tile", tiles, late_sums_one, late)
    late = reduce_start("slab", slabs, late_sums_two, two_send.at[1], two_recv.at[1])
    for copy in late:
        copy.start()
    gram_ref[RANK:] = reduce_end("slab", slabs, late_sums_two, late)

    for k in range(SNAPS):
        for d in range(1, tiles):
            bulk(k, d).wait_send()


def mix(row_scale, low, sigma_ref, rotation_ref, factor_ref, weight_ref, snap_ref):
    rows = GRAM_ROWS
    row = iota((rows, LANES), 0)
    lane = iota((rows, LANES), 1)
    weight = jnp.where(iota((1, LANES), 1) < RANK, sigma_ref[...], 1.0)
    wide_weight = jnp.broadcast_to(weight, (LANES, LANES))
    low = low * weight * wide_weight.T[:rows]
    high = jnp.concatenate([low, jnp.zeros((LANES - rows, LANES), F32)], axis=0).T[:rows]
    gram = jnp.where((row < RANK) & (lane >= RANK), high, low)
    upper_right = (row >= RANK) & (lane > row)
    gram = jnp.where(upper_right, high, gram)
    gram = jnp.where((lane < K) & (row < K), gram, 0.0)
    start = gram + jnp.where((lane == row + 64) | ((lane == row) & (row >= K)), 1.0, 0.0)
    blocks = [start[SUB * b : SUB * b + SUB] for b in range(rows // SUB)]
    sub = iota((SUB, LANES), 0)
    for i in range(K):
        at, inner = divmod(i, SUB)
        pivot_row = blocks[at][inner : inner + 1, :]
        scaled = pivot_row / pivot_row[:, i : i + 1]
        for b in range(at, rows // SUB):
            column = blocks[b][:, i : i + 1]
            update = column * scaled
            if b == at:
                update = jnp.where(sub > inner, update, 0.0)
            blocks[b] = blocks[b] - update
    done = jnp.concatenate(blocks, axis=0)
    pivots = jnp.sum(jnp.where(lane == row, done, 0.0), axis=1, keepdims=True)
    done = done / jnp.sqrt(pivots)
    factor = jnp.where(lane >= row, done, 0.0) * (1.0 / row_scale)
    factor_ref[...] = factor[:K, :K]
    inverse = jnp.where(row < K, done, 0.0)
    mixed = row_scale * lax.dot_general(
        rotation_ref[...],
        inverse,
        (((0,), (0,)), ((), ())),
        precision=HIGHEST,
        preferred_element_type=F32,
    )
    mixed = mixed[:RANK]
    sigma_lane = jnp.concatenate([jnp.zeros((1, 64), F32), sigma_ref[:, :64]], axis=1)
    spread = ((iota((LANES, WIDE), 0) - 64) == iota((LANES, WIDE), 1) // SUB).astype(BF16)
    same = iota((WIDE, WIDE), 0) % SUB == iota((WIDE, WIDE), 1) % SUB
    for part, values in enumerate(pieces(mixed * sigma_lane, 2)):
        wide = jnp.dot(values, spread, preferred_element_type=F32)
        tall = jnp.broadcast_to(wide[:, None, :], (RANK, SUB, WIDE)).reshape(WIDE, WIDE)
        weight_ref[WIDE * part : WIDE * part + WIDE] = jnp.where(same, tall, 0.0).astype(BF16)
    for s in range(SNAPS):
        column = mixed[:, 64 + RANK + s : 64 + RANK + s + 1]
        snap_ref[s] = jnp.broadcast_to(column[:, :, None], (RANK, SUB, LANES))


def rotate_kernel(
    row_scale,
    gram_ref,
    sigma_ref,
    rotation_ref,
    modes_hbm,
    snaps,
    flow,
    advanced,
    factor_ref,
    new_modes,
    modes,
    weight_ref,
    snap_ref,
    staged,
    flow_sem,
    out_sem,
    mode_sem,
):
    planes, tiles = modes.shape[1], modes.shape[2]

    def mode_copy(plane):
        return pltpu.make_async_copy(modes_hbm.at[:, plane], modes.at[:, plane], mode_sem.at[plane])

    for plane in range(planes):
        mode_copy(plane).start()
    passing = pltpu.make_async_copy(flow, advanced, flow_sem)
    passing.start()
    mix(row_scale, gram_ref[...], sigma_ref, rotation_ref, factor_ref, weight_ref, snap_ref)
    width = snaps.shape[2]

    def out_copy(plane, slot):
        return pltpu.make_async_copy(staged.at[slot], new_modes.at[:, plane], out_sem.at[slot])

    def plane_step(plane, carry):
        slot = lax.rem(plane, 2)

        @pl.when(plane >= 2)
        def _():
            out_copy(plane - 2, slot).wait()

        mode_copy(plane).wait()
        c, w = lax.div(plane, width), lax.rem(plane, width)
        for t in range(0, tiles, 2):
            both = jnp.dot(weight_ref[...], wide_pair(modes, plane, t), preferred_element_type=F32)
            both = both[:WIDE] + both[WIDE:]
            for half in range(2):
                value = both[:, LANES * half : LANES * half + LANES].reshape(RANK, SUB, LANES)
                for s in range(SNAPS):
                    value = value + snap_ref[s] * snaps[s, c, w, t + half][None]
                staged[slot, :, t + half] = value.astype(BF16)
        out_copy(plane, slot).start()
        return carry

    lax.fori_loop(0, planes, plane_step, 0)
    for plane in (planes - 2, planes - 1):
        out_copy(plane, plane % 2).wait()
    passing.wait()


def hbm_spec():
    return pl.BlockSpec(memory_space=pltpu.HBM)


def vmem_spec():
    return pl.BlockSpec(memory_space=pltpu.VMEM)


def shards(slabs, tiles, velocity, viscosity, basis, sigma, rotation):
    _, parts, width, deep, lanes = basis.shape
    planes, deep_tiles = parts * width, deep // SUB
    count = velocity.shape[1]
    row_scale = math.sqrt(planes * deep * lanes * slabs * tiles)
    modes_hbm = basis.reshape(RANK, planes, deep_tiles, SUB, LANES)
    flow_shape = (3, count, 2, SUB, LANES)
    flow, gram, snaps = pl.pallas_call(
        functools.partial(exchange_kernel, slabs, tiles),
        in_specs=[hbm_spec(), hbm_spec(), hbm_spec()],
        out_specs=[vmem_spec(), vmem_spec(), vmem_spec()],
        out_shape=[
            pltpu.VMEM(flow_shape, F32),
            pltpu.VMEM((GRAM_ROWS, LANES), F32),
            pltpu.VMEM((SNAPS, parts, width, deep_tiles, SUB, LANES), F32),
        ],
        scratch_shapes=[
            pltpu.VMEM(modes_hbm.shape, BF16),
            pltpu.VMEM((2, 3, count + 2, 2, SUB, LANES), F32),
            pltpu.VMEM((count, 2, SUB, LANES), F32),
            pltpu.VMEM((2, 3, count, LANES), F32),
            pltpu.VMEM((2, 3, count, LANES), F32),
            pltpu.VMEM((2, 3, count, LANES), F32),
            pltpu.VMEM((2, 3, count, LANES), F32),
            pltpu.VMEM((WIDE, WIDE), F32),
            pltpu.VMEM((9, SUB, LANES), F32),
            pltpu.VMEM((1 + tiles, RANK, LANES), F32),
            pltpu.VMEM((1 + slabs, RANK, LANES), F32),
            pltpu.VMEM((1 + tiles, SUB, LANES), F32),
            pltpu.VMEM((1 + slabs, SUB, LANES), F32),
            pltpu.SemaphoreType.DMA((2,)),
            pltpu.SemaphoreType.DMA((planes,)),
            pltpu.SemaphoreType.DMA((SNAPS,)),
            pltpu.SemaphoreType.DMA((2, 4)),
            pltpu.SemaphoreType.DMA((2, 4)),
            pltpu.SemaphoreType.DMA((SNAPS, tiles)),
            pltpu.SemaphoreType.DMA((SNAPS, tiles)),
            pltpu.SemaphoreType.DMA((2, tiles)),
            pltpu.SemaphoreType.DMA((2, tiles)),
            pltpu.SemaphoreType.DMA((2, slabs)),
            pltpu.SemaphoreType.DMA((2, slabs)),
        ],
        compiler_params=pltpu.CompilerParams(
            collective_id=0, has_side_effects=True, vmem_limit_bytes=EXCHANGE_VMEM
        ),
        name="exchange",
    )(velocity.reshape(flow_shape), viscosity.reshape(count, 2, SUB, LANES), modes_hbm)
    sigma_row = jnp.pad(sigma[None], ((0, 0), (0, LANES - RANK)))
    rotation_wide = jnp.pad(rotation, ((0, GRAM_ROWS - K), (0, LANES - RANK)))
    advanced, factor, rotated = pl.pallas_call(
        functools.partial(rotate_kernel, row_scale),
        in_specs=[vmem_spec(), vmem_spec(), vmem_spec(), hbm_spec(), vmem_spec(), vmem_spec()],
        out_specs=[hbm_spec(), vmem_spec(), hbm_spec()],
        out_shape=[
            jax.ShapeDtypeStruct(flow_shape, F32),
            jax.ShapeDtypeStruct((K, K), F32),
            jax.ShapeDtypeStruct(modes_hbm.shape, BF16),
        ],
        scratch_shapes=[
            pltpu.VMEM(modes_hbm.shape, BF16),
            pltpu.VMEM((2 * WIDE, WIDE), BF16),
            pltpu.VMEM((SNAPS, RANK, SUB, LANES), F32),
            pltpu.VMEM((2, RANK, deep_tiles, SUB, LANES), BF16),
            pltpu.SemaphoreType.DMA,
            pltpu.SemaphoreType.DMA((2,)),
            pltpu.SemaphoreType.DMA((planes,)),
        ],
        compiler_params=pltpu.CompilerParams(vmem_limit_bytes=ROTATE_VMEM),
        name="rotate",
    )(gram, sigma_row, rotation_wide, modes_hbm, snaps, flow)
    return (advanced.reshape(velocity.shape), factor, rotated.reshape(basis.shape))


def solution(mesh):
    in_specs = (
        P(None, "slab", "tile", None),
        P("slab", "tile", None),
        P(None, None, ("slab", "tile"), None, None),
        P(),
        P(),
    )
    out_specs = (P(None, "slab", "tile", None), P(), P(None, None, ("slab", "tile"), None, None))
    return jax.shard_map(
        functools.partial(shards, mesh.shape["slab"], mesh.shape["tile"]),
        mesh=mesh,
        in_specs=in_specs,
        out_specs=out_specs,
        check_vma=False,
    )
```

time: 174 us -> 80.4 us (0.46)
  blocking collectives: 64.7 us -> 0 us
  Pallas kernels: 47.3 us -> 78.1 us
  waiting for transfers between devices: 29.7 us -> 0 us
  starting transfers between devices: 17 us -> 0 us
  local copies, waits for them, and re-layouts: 7.6 us -> 1.47 us
  other arithmetic: 5.9 us -> 0 us
    psum x1 -> x0, blocking collectives: 64.7 us -> none  [shards(): lax.psum(jnp.concatenate([basis_gram, snap_gram], axis=0), ('slab', 'tile'))]
    pallas_call x4 -> x2, Pallas kernels: 47.3 us -> 78.1 us  [the longest x1 61.3 us: shards(): pl.pallas_call(functools.partial(exchange_kernel, slabs, tiles), in_specs...]
    ppermute x8 -> x0, waiting for transfers between devices: 17.1 us -> none  [the longest x4 9.1 us: extended(): lax.ppermute(lax.slice_in_dim(block, 0, width, axis=dim), axis, backward)]
    ppermute x8 -> x0, starting transfers between devices: 13.2 us -> none  [the longest x4 9.18 us: extended(): lax.ppermute(lax.slice_in_dim(block, block.shape[dim] - width, None, axis...]
    all_to_all x1 -> x0, waiting for transfers between devices: 12.7 us -> none  [shards(): lax.all_to_all(jnp.stack(history), 'tile', split_axis=2, concat_axis=3, t...]
    all_to_all x1 -> x0, starting transfers between devices: 3.76 us -> none  [shards(): lax.all_to_all(jnp.stack(history), 'tile', split_axis=2, concat_axis=3, t...]
    add x2 -> x0, other arithmetic: 2.67 us -> none  [advance(): return centre + step_size * (viscosity * laplace - 0.5 * carried)]
    another operation x2 -> x0, other arithmetic: 2.46 us -> none  [shards(): jnp.stack(history)]
  transfers between devices with their start and end apart: 9 -> 0, of which waited for: 9 -> 0; matrix products, arithmetic and copies ran while one was open for 3% -> 0% of each run, Pallas kernels for 7% -> 0%
where the time goes in v2:
time: 80.4 us; the launch traced here: 80.2 us
  Pallas kernels  78.1 us (97%)
  local copies, waits for them, and re-layouts  1.47 us (2%)
    pallas_call x1, Pallas kernels, shards(): pl.pallas_call(functools.partial(exchange_kernel, slabs, tiles), in_specs...  61.3 us
    pallas_call x1, Pallas kernels, shards(): pl.pallas_call(functools.partial(rotate_kernel, row_scale), in_specs=[vme...  16.7 us

profile of v2, /device:TPU:1, one launch (start us, length us, event | category | flops | bytes accessed | tf_op | source)
XLA Modules:
  0.0 80.2 jit_solution(2474510757888065735)
XLA Ops:
  0.6 0.7 pad.8.sigma_ref
  1.3 0.8 copy.8
  2.1 61.3 %exchange.1 = (f32[3,32,2,8,128]{4,3,2,1,0:T(8,128)S(1)}, f32[40,128]{1,0:T(8,128)S(1)}, f32[3,3,4,16,8,128]{5,4,3,2,1,0:T(8,128)S(1)}) custom-call(f32[3,32,2,8,128]{4,3,2,1,0:T(8,128)} %bitcast.8, f32[32,2,8,128]{3,2,1,0:T(8,128)} %bitcast.9, bf16[32,12,16,8,128]{4,3,2,1,0:T(8,128)(2,1)} %bitcast.6), custom_call_target="tpu_custom_call" | custom-call | tf_op jit(solution)/shard_map/exchange/pallas_call | solution.py:480
  63.5 16.7 %rotate.1 = (f32[3,32,2,8,128]{4,3,2,1,0:T(8,128)}, f32[35,35]{1,0:T(8,128)}, bf16[32,12,16,8,128]{4,3,2,1,0:T(8,128)(2,1)}) custom-call(f32[40,128]{1,0:T(8,128)S(1)} %get-tuple-element.9.gram_ref, f32[1,128]{1,0:T(1,128)S(1)} %pad.8.sigma_ref, f32[40,128]{1,0:T(8,128)S(1)} %pad.9.rotation_ref, bf16[32,12,16,8,128]{4,3,2,1,0:T(8,128)(2,1)} %bitcast.7, ...), custom_call_target="tpu_custom_call" | custom-call | tf_op jit(solution)/shard_map/rotate/pallas_call | solution.py:522
  (1 shorter events, 0.0 us)

commit v3 on v2

--- a/solution.py
+++ b/solution.py
@@ -88,8 +88,10 @@
     vel_hbm,
     nu_hbm,
     modes_hbm,
+    sigma_ref,
     advanced,
-    gram_ref,
+    early_ref,
+    late_ref,
     snaps,
     modes,
     flow,
@@ -104,6 +106,7 @@
     sums_two,
     late_sums_one,
     late_sums_two,
+    weight_row,
     load_sem,
     mode_sem,
     own_sem,
@@ -213,36 +216,6 @@
 
         lax.fori_loop(first, last, plane_step, 0)
 
-    first_faces = faces(0)
-    for copy in first_faces:
-        copy.start()
-    send_strips(0)
-    products[...] = jnp.zeros_like(products)
-    squares[...] = jnp.zeros_like(squares)
-    gram_planes(0, planes // 2)
-    for copy in first_faces:
-        copy.wait()
-
-    def store_first(c, x, value):
-        flow[1, c, x + 1] = value.reshape(2, SUB, LANES)
-        low_edge[1, c, pl.ds(x, 1)] = value[0:1]
-        high_edge[1, c, pl.ds(x, 1)] = value[2 * SUB - 1 :]
-
-    advance_planes(flow.at[0], low.at[0], high.at[0], nu, store_first)
-    second_faces = faces(1)
-    for copy in second_faces:
-        copy.start()
-    send_strips(1)
-    gram_planes(planes // 2, planes)
-    for copy in second_faces:
-        copy.wait()
-
-    def store_second(c, x, value):
-        advanced[c, x] = value.reshape(2, SUB, LANES)
-
-    advance_planes(flow.at[1], low.at[1], high.at[1], nu, store_second)
-    send_strips(2)
-
     def reduce_start(axis, size, sums, send, recv):
         me = lax.axis_index(axis)
         return [
@@ -267,75 +240,128 @@
             total = total + sums[1 + i]
         return total
 
+    first_faces = faces(0)
+    for copy in first_faces:
+        copy.start()
+    send_strips(0)
+    weight_row[...] = jnp.zeros_like(weight_row)
+    weight_row[:, :RANK] = sigma_ref[...]
+    products[...] = jnp.zeros_like(products)
+    squares[...] = jnp.zeros_like(squares)
+    gram_planes(0, planes)
     sums_one[0] = matched(products[...], RANK)
     basis_one = reduce_start("tile", tiles, sums_one, one_send.at[0], one_recv.at[0])
     for copy in basis_one:
         copy.start()
-
-    snap_rows = 3 * SNAPS * SUB
-    products[:snap_rows] = jnp.zeros((snap_rows, WIDE), F32)
-
-    def piece(d, carry):
-        @pl.when(d == 0)
-        def _():
-            for k in range(SNAPS):
-                own(k).wait()
-
-        @pl.when(d > 0)
-        def _():
-            for k in range(SNAPS):
-                bulk(k, d).wait_recv()
-
-        at = 2 * shifted(tile, -d, tiles)
-        columns = jnp.concatenate([wide_pair(modes, p, at) for p in range(planes)], axis=1)
-        rows = []
-        for k in range(SNAPS):
-            flat = jnp.concatenate(
-                [
-                    snaps[k, p // width, p % width, at + h]
-                    for p in range(planes)
-                    for h in range(2)
-                ],
-                axis=1,
-            )
-            rows.extend(pieces(flat, 3))
-        products[:snap_rows] += lax.dot_general(
-            jnp.concatenate(rows, axis=0),
-            columns,
-            (((1,), (1,)), ((), ())),
-            preferred_element_type=F32,
-        )
-        for a in range(SNAPS):
-            for b in range(a + 1):
-                total = jnp.zeros((SUB, LANES), F32)
-                for p in range(planes):
-                    for h in range(2):
-                        c, w = divmod(p, width)
-                        total = total + snaps[a, c, w, at + h] * snaps[b, c, w, at + h]
-                squares[3 * a + b] += total
-        return carry
-
-    lax.fori_loop(0, tiles // 2, piece, 0)
+    for copy in first_faces:
+        copy.wait()
+
+    def store_first(c, x, value):
+        flow[1, c, x + 1] = value.reshape(2, SUB, LANES)
+        low_edge[1, c, pl.ds(x, 1)] = value[0:1]
+        high_edge[1, c, pl.ds(x, 1)] = value[2 * SUB - 1 :]
+
+    advance_planes(flow.at[0], low.at[0], high.at[0], nu, store_first)
+    second_faces = faces(1)
+    for copy in second_faces:
+        copy.start()
+    send_strips(1)
     sums_two[0] = reduce_end("tile", tiles, sums_one, basis_one)
     basis_two = reduce_start("slab", slabs, sums_two, two_send.at[0], two_recv.at[0])
     for copy in basis_two:
         copy.start()
-    lax.fori_loop(tiles // 2, tiles, piece, 0)
-    gram_ref[:RANK] = reduce_end("slab", slabs, sums_two, basis_two)
+    for copy in second_faces:
+        copy.wait()
+
+    def store_second(c, x, value):
+        advanced[c, x] = value.reshape(2, SUB, LANES)
+
+    advance_planes(flow.at[1], low.at[1], high.at[1], nu, store_second)
+    send_strips(2)
+
+    weight = weight_row[...]
+    early_row = iota((RANK, LANES), 0)
+    early_lane = iota((RANK, LANES), 1)
+    tall_weight = jnp.broadcast_to(weight, (LANES, LANES)).T[:RANK]
+    early_ref[...] = reduce_end("slab", slabs, sums_two, basis_two) * weight * tall_weight + (
+        early_lane == early_row + 64
+    ).astype(F32)
+
+    def eliminate(i, carry):
+        block = early_ref[...]
+        pivot_row = early_ref[pl.ds(i, 1)]
+        column = jnp.sum(jnp.where(early_lane == i, block, 0.0), axis=1, keepdims=True)
+        pivot = jnp.sum(jnp.where(early_lane[:1] == i, pivot_row, 0.0), axis=1, keepdims=True)
+        update = column * (pivot_row / pivot)
+        early_ref[...] = block - jnp.where(early_row > i, update, 0.0)
+        return carry
+
+    lax.fori_loop(0, RANK, eliminate, 0)
+    eliminated = early_ref[...]
+    pivots = jnp.sum(jnp.where(early_lane == early_row, eliminated, 0.0), axis=1, keepdims=True)
+    eliminated = eliminated / jnp.sqrt(pivots)
+    early_ref[...] = jnp.where((early_lane >= early_row) | (early_lane >= 64), eliminated, 0.0)
+
+    snap_rows = 3 * SNAPS * SUB
+    products[:snap_rows] = jnp.zeros((snap_rows, WIDE), F32)
+
+    def gram_pieces(group):
+        def piece(turn, carry):
+            @pl.when(turn == 0)
+            def _():
+                for k in group:
+                    own(k).wait()
+
+            @pl.when(turn > 0)
+            def _():
+                for k in group:
+                    bulk(k, turn).wait_recv()
+
+            at = 2 * shifted(tile, -turn, tiles)
+            columns = jnp.concatenate([wide_pair(modes, p, at) for p in range(planes)], axis=1)
+            rows = []
+            for k in group:
+                flat = jnp.concatenate(
+                    [
+                        snaps[k, p // width, p % width, at + h]
+                        for p in range(planes)
+                        for h in range(2)
+                    ],
+                    axis=1,
+                )
+                rows.extend(pieces(flat, 3))
+            first, last = 3 * SUB * group[0], 3 * SUB * (group[-1] + 1)
+            products[first:last] += lax.dot_general(
+                jnp.concatenate(rows, axis=0),
+                columns,
+                (((1,), (1,)), ((), ())),
+                preferred_element_type=F32,
+            )
+            for a in group:
+                for b in range(a + 1):
+                    total = jnp.zeros((SUB, LANES), F32)
+                    for p in range(planes):
+                        for h in range(2):
+                            c, w = divmod(p, width)
+                            total = total + snaps[a, c, w, at + h] * snaps[b, c, w, at + h]
+                    squares[3 * a + b] += total
+            return carry
+
+        lax.fori_loop(0, tiles, piece, 0)
+
+    gram_pieces((0, 1))
+    gram_pieces((2,))
     by_part = matched(products[:snap_rows], 3 * SNAPS)
-    lines = [
-        by_part[3 * s : 3 * s + 1] + by_part[3 * s + 1 : 3 * s + 2] + by_part[3 * s + 2 : 3 * s + 3]
-        for s in range(SNAPS)
-    ]
-
     row = iota((SUB, LANES), 0)
     lane = iota((SUB, LANES), 1)
     result = jnp.zeros((SUB, LANES), F32)
     for s in range(SNAPS):
-        result = jnp.where(row == s, lines[s], result)
+        line = by_part[3 * s : 3 * s + 1] + by_part[3 * s + 1 : 3 * s + 2] + by_part[3 * s + 2 : 3 * s + 3]
+        result = jnp.where(row == s, line, result)
     for a in range(SNAPS):
         for b in range(a + 1):
-            result = jnp.where((row == a) & (lane == RANK + b), jnp.sum(squares[3 * a + b]), result)
+            here = ((row == a) & (lane == RANK + b)) | ((row == b) & (lane == RANK + a))
+            result = jnp.where(here, jnp.sum(squares[3 * a + b]), result)
     late_sums_one[0] = result
     late = reduce_start("tile", tiles, late_sums_one, one_send.at[1], one_recv.at[1])
     for copy in late:
@@ -344,53 +370,50 @@
     late = reduce_start("slab", slabs, late_sums_two, two_send.at[1], two_recv.at[1])
     for copy in late:
         copy.start()
-    gram_ref[RANK:] = reduce_end("slab", slabs, late_sums_two, late)
+    late_ref[...] = reduce_end("slab", slabs, late_sums_two, late)
 
     for k in range(SNAPS):
         for d in range(1, tiles):
             bulk(k, d).wait_send()
 
 
-def mix(row_scale, low, sigma_ref, rotation_ref, factor_ref, weight_ref, snap_ref):
-    rows = GRAM_ROWS
-    row = iota((rows, LANES), 0)
-    lane = iota((rows, LANES), 1)
-    weight = jnp.where(iota((1, LANES), 1) < RANK, sigma_ref[...], 1.0)
-    wide_weight = jnp.broadcast_to(weight, (LANES, LANES))
-    low = low * weight * wide_weight.T[:rows]
-    high = jnp.concatenate([low, jnp.zeros((LANES - rows, LANES), F32)], axis=0).T[:rows]
-    gram = jnp.where((row < RANK) & (lane >= RANK), high, low)
-    upper_right = (row >= RANK) & (lane > row)
-    gram = jnp.where(upper_right, high, gram)
-    gram = jnp.where((lane < K) & (row < K), gram, 0.0)
-    start = gram + jnp.where((lane == row + 64) | ((lane == row) & (row >= K)), 1.0, 0.0)
-    blocks = [start[SUB * b : SUB * b + SUB] for b in range(rows // SUB)]
+def mix(row_scale, early_ref, late_ref, sigma_row, rotation_ref, factor_ref, weight_ref, snap_ref):
+    row = iota((GRAM_ROWS, LANES), 0)
+    lane = iota((GRAM_ROWS, LANES), 1)
     sub = iota((SUB, LANES), 0)
-    for i in range(K):
-        at, inner = divmod(i, SUB)
-        pivot_row = blocks[at][inner : inner + 1, :]
-        scaled = pivot_row / pivot_row[:, i : i + 1]
-        for b in range(at, rows // SUB):
-            column = blocks[b][:, i : i + 1]
-            update = column * scaled
-            if b == at:
-                update = jnp.where(sub > inner, update, 0.0)
-            blocks[b] = blocks[b] - update
-    done = jnp.concatenate(blocks, axis=0)
-    pivots = jnp.sum(jnp.where(lane == row, done, 0.0), axis=1, keepdims=True)
-    done = done / jnp.sqrt(pivots)
+    short = iota((SUB, LANES), 1)
+    top = early_ref[...]
+    inverse_top = jnp.where(lane[:RANK] >= 64, top, 0.0)
+    late = late_ref[...] * jnp.where(short < RANK, sigma_row, 1.0)
+    cross = pltpu.roll(jnp.where(short < RANK, late, 0.0), 64, 1)
+    placed = jnp.concatenate(
+        [jnp.zeros((RANK, LANES), F32), cross, jnp.zeros((LANES - GRAM_ROWS, LANES), F32)], axis=0
+    )
+    lanes_both = (((1,), (1,)), ((), ()))
+    top = top + lax.dot_general(
+        inverse_top, placed, lanes_both, precision=HIGHEST, preferred_element_type=F32
+    )
+    weights = lax.dot_general(
+        cross, inverse_top, lanes_both, precision=HIGHEST, preferred_element_type=F32
+    )
+    bottom = jnp.where(sub < SNAPS, late, 0.0) + (
+        (short == sub + 64 + RANK) | ((short == sub + RANK) & (sub >= SNAPS))
+    ).astype(F32)
+    bottom = bottom - jnp.dot(weights, top, precision=HIGHEST, preferred_element_type=F32)
+    for i in range(SNAPS):
+        pivot_row = bottom[i : i + 1]
+        scaled = pivot_row / pivot_row[:, RANK + i : RANK + i + 1]
+        update = bottom[:, RANK + i : RANK + i + 1] * scaled
+        bottom = bottom - jnp.where(sub > i, update, 0.0)
+    pivots = jnp.sum(jnp.where(short == sub + RANK, bottom, 0.0), axis=1, keepdims=True)
+    done = jnp.concatenate([top, bottom / jnp.sqrt(pivots)], axis=0)
     factor = jnp.where(lane >= row, done, 0.0) * (1.0 / row_scale)
     factor_ref[...] = factor[:K, :K]
     inverse = jnp.where(row < K, done, 0.0)
-    mixed = row_scale * lax.dot_general(
-        rotation_ref[...],
-        inverse,
-        (((0,), (0,)), ((), ())),
-        precision=HIGHEST,
-        preferred_element_type=F32,
-    )
-    mixed = mixed[:RANK]
-    sigma_lane = jnp.concatenate([jnp.zeros((1, 64), F32), sigma_ref[:, :64]], axis=1)
+    mixed = row_scale * jnp.dot(
+        rotation_ref[:, :GRAM_ROWS], inverse, precision=HIGHEST, preferred_element_type=F32
+    )
+    sigma_lane = pltpu.roll(sigma_row, 64, 1)
     spread = ((iota((LANES, WIDE), 0) - 64) == iota((LANES, WIDE), 1) // SUB).astype(BF16)
     same = iota((WIDE, WIDE), 0) % SUB == iota((WIDE, WIDE), 1) % SUB
     for part, values in enumerate(pieces(mixed * sigma_lane, 2)):
@@ -404,7 +427,8 @@
 
 def rotate_kernel(
     row_scale,
-    gram_ref,
+    early_ref,
+    late_ref,
     sigma_ref,
     rotation_ref,
     modes_hbm,
@@ -414,6 +438,8 @@
     factor_ref,
     new_modes,
     modes,
+    sigma_row,
+    rotation_wide,
     weight_ref,
     snap_ref,
     staged,
@@ -430,7 +456,13 @@
         mode_copy(plane).start()
     passing = pltpu.make_async_copy(flow, advanced, flow_sem)
     passing.start()
-    mix(row_scale, gram_ref[...], sigma_ref, rotation_ref, factor_ref, weight_ref, snap_ref)
+    sigma_row[...] = jnp.zeros_like(sigma_row)
+    sigma_row[:, :RANK] = sigma_ref[...]
+    rotation_wide[...] = jnp.zeros_like(rotation_wide)
+    rotation_wide[:, :K] = rotation_ref[...]
+    mix(
+        row_scale, early_ref, late_ref, sigma_row[...], rotation_wide, factor_ref, weight_ref, snap_ref
+    )
     width = snaps.shape[2]
 
     def out_copy(plane, slot):
@@ -477,13 +509,15 @@
     row_scale = math.sqrt(planes * deep * lanes * slabs * tiles)
     modes_hbm = basis.reshape(RANK, planes, deep_tiles, SUB, LANES)
     flow_shape = (3, count, 2, SUB, LANES)
-    flow, gram, snaps = pl.pallas_call(
+    sigma_row = sigma.reshape(1, RANK)
+    flow, early, late, snaps = pl.pallas_call(
         functools.partial(exchange_kernel, slabs, tiles),
-        in_specs=[hbm_spec(), hbm_spec(), hbm_spec()],
-        out_specs=[vmem_spec(), vmem_spec(), vmem_spec()],
+        in_specs=[hbm_spec(), hbm_spec(), hbm_spec(), vmem_spec()],
+        out_specs=[vmem_spec()] * 4,
         out_shape=[
             pltpu.VMEM(flow_shape, F32),
-            pltpu.VMEM((GRAM_ROWS, LANES), F32),
+            pltpu.VMEM((RANK, LANES), F32),
+            pltpu.VMEM((SUB, LANES), F32),
             pltpu.VMEM((SNAPS, parts, width, deep_tiles, SUB, LANES), F32),
         ],
         scratch_shapes=[
@@ -500,6 +534,7 @@
             pltpu.VMEM((1 + slabs, RANK, LANES), F32),
             pltpu.VMEM((1 + tiles, SUB, LANES), F32),
             pltpu.VMEM((1 + slabs, SUB, LANES), F32),
+            pltpu.VMEM((1, LANES), F32),
             pltpu.SemaphoreType.DMA((2,)),
             pltpu.SemaphoreType.DMA((planes,)),
             pltpu.SemaphoreType.DMA((SNAPS,)),
@@ -516,12 +551,10 @@
             collective_id=0, has_side_effects=True, vmem_limit_bytes=EXCHANGE_VMEM
         ),
         name="exchange",
-    )(velocity.reshape(flow_shape), viscosity.reshape(count, 2, SUB, LANES), modes_hbm)
-    sigma_row = jnp.pad(sigma[None], ((0, 0), (0, LANES - RANK)))
-    rotation_wide = jnp.pad(rotation, ((0, GRAM_ROWS - K), (0, LANES - RANK)))
+    )(velocity.reshape(flow_shape), viscosity.reshape(count, 2, SUB, LANES), modes_hbm, sigma_row)
     advanced, factor, rotated = pl.pallas_call(
         functools.partial(rotate_kernel, row_scale),
-        in_specs=[vmem_spec(), vmem_spec(), vmem_spec(), hbm_spec(), vmem_spec(), vmem_spec()],
+        in_specs=[vmem_spec()] * 4 + [hbm_spec(), vmem_spec(), vmem_spec()],
         out_specs=[hbm_spec(), vmem_spec(), hbm_spec()],
         out_shape=[
             jax.ShapeDtypeStruct(flow_shape, F32),
@@ -530,6 +563,8 @@
         ],
         scratch_shapes=[
             pltpu.VMEM(modes_hbm.shape, BF16),
+            pltpu.VMEM((1, LANES), F32),
+            pltpu.VMEM((RANK, LANES), F32),
             pltpu.VMEM((2 * WIDE, WIDE), BF16),
             pltpu.VMEM((SNAPS, RANK, SUB, LANES), F32),
             pltpu.VMEM((2, RANK, deep_tiles, SUB, LANES), BF16),
@@ -539,7 +574,7 @@
         ],
         compiler_params=pltpu.CompilerParams(vmem_limit_bytes=ROTATE_VMEM),
         name="rotate",
-    )(gram, sigma_row, rotation_wide, modes_hbm, snaps, flow)
+    )(early, late, sigma_row, rotation.T, modes_hbm, snaps, flow)
     return (advanced.reshape(velocity.shape), factor, rotated.reshape(basis.shape))
 
 

time: 80.4 us -> 76.7 us (0.954)
  Pallas kernels: 78.1 us -> 75.8 us
  local copies, waits for them, and re-layouts: 1.47 us -> 0.01 us
    pallas_call x1, Pallas kernels: 16.7 us -> 14.3 us  [shards(): pl.pallas_call(functools.partial(rotate_kernel, row_scale), in_specs=[vme...]
where the time goes in v3:
time: 76.7 us; the launch traced here: 76.5 us
  Pallas kernels  75.8 us (99%)
    pallas_call x1, Pallas kernels, shards(): pl.pallas_call(functools.partial(exchange_kernel, slabs, tiles), in_specs...  61.5 us
    pallas_call x1, Pallas kernels, shards(): pl.pallas_call(functools.partial(rotate_kernel, row_scale), in_specs=[vme...  14.3 us

profile of v3, /device:TPU:1, one launch (start us, length us, event | category | flops | bytes accessed | tf_op | source)
XLA Modules:
  0.0 76.5 jit_solution(7356497878530125666)
XLA Ops:
  0.6 0.0 copy-start
  0.6 0.0 copy-start.1
  0.7 61.5 %exchange.1 = (f32[3,32,2,8,128]{4,3,2,1,0:T(8,128)S(1)}, f32[32,128]{1,0:T(8,128)S(1)}, f32[8,128]{1,0:T(8,128)S(1)}, f32[3,3,4,16,8,128]{5,4,3,2,1,0:T(8,128)S(1)}) custom-call(f32[3,32,2,8,128]{4,3,2,1,0:T(8,128)} %bitcast.12, f32[32,2,8,128]{3,2,1,0:T(8,128)} %bitcast.13, bf16[32,12,16,8,128]{4,3,2,1,0:T(8,128)(2,1)} %bitcast.10, f32[1,32]{1,0:T(1,128)} %bitcast.8), custom_call_target="tpu_custom_call" | custom-call | tf_op jit(solution)/shard_map/exchange/pallas_call | solution.py:513
  62.2 0.0 copy-done
  62.2 0.0 copy-done.1
  62.2 14.3 %rotate.1 = (f32[3,32,2,8,128]{4,3,2,1,0:T(8,128)}, f32[35,35]{1,0:T(8,128)}, bf16[32,12,16,8,128]{4,3,2,1,0:T(8,128)(2,1)}) custom-call(f32[32,128]{1,0:T(8,128)S(1)} %get-tuple-element.10.early_ref, f32[8,128]{1,0:T(8,128)S(1)} %get-tuple-element.11.late_ref, f32[1,32]{1,0:T(1,128)S(1)} %bitcast.9, f32[32,35]{1,0:T(8,128)S(1)} %bitcast.7, ...), custom_call_target="tpu_custom_call" | custom-call | tf_op jit(solution)/shard_map/rotate/pallas_call | solution.py:555
Async XLA Ops:
  0.6 61.5 %copy-start = (f32[35,32]{0,1:T(8,128)S(1)}, f32[35,32]{0,1:T(8,128)}, u32[]{:S(2)}) copy-start(f32[35,32]{0,1:T(8,128)} %param.9) | copy-start | bytes 13444
  0.6 61.5 %copy-start.1 = (f32[32]{0:T(128)S(1)}, f32[32]{0:T(128)}, u32[]{:S(2)}) copy-start(f32[32]{0:T(128)} %param.8) | copy-start | bytes 388

commit v4 on v3

--- a/solution.py
+++ b/solution.py
@@ -20,6 +20,8 @@
 HIGHEST = lax.Precision.HIGHEST
 MESH = pl.DeviceIdType.MESH
 GRAM_ROWS = 40
+CORES = 2
+HALVES = 2
 EXCHANGE_VMEM = 63_700_000
 ROTATE_VMEM = 50 << 20
 
@@ -127,6 +129,19 @@
     def shifted(index, by, size):
         return lax.rem(index + by + size, size)
 
+    block = HALVES * CORES
+    near, far = slabs // HALVES, HALVES * tiles
+    line, half, core = lax.div(slab, block), lax.rem(lax.div(slab, CORES), HALVES), lax.rem(slab, CORES)
+    near_me, far_me = line * CORES + core, half * tiles + tile
+
+    def near_peer(d):
+        peer = shifted(near_me, d, near)
+        return {"slab": lax.div(peer, CORES) * block + half * CORES + lax.rem(peer, CORES)}
+
+    def far_peer(d):
+        peer = shifted(far_me, d, far)
+        return {"slab": line * block + lax.div(peer, tiles) * CORES + core, "tile": lax.rem(peer, tiles)}
+
     loads = [
         pltpu.make_async_copy(vel_hbm, flow.at[0, :, 1 : count + 1], load_sem.at[0]),
         pltpu.make_async_copy(nu_hbm, nu, load_sem.at[1]),
@@ -135,10 +150,13 @@
         copy.start()
 
     barrier = pltpu.get_barrier_semaphore()
-    for d in range(1, tiles):
-        pl.semaphore_signal(barrier, inc=1, device_id={"tile": shifted(tile, d, tiles)}, device_id_type=MESH)
-    for d in range(1, slabs):
-        pl.semaphore_signal(barrier, inc=1, device_id={"slab": shifted(slab, d, slabs)}, device_id_type=MESH)
+    greeted = [{"slab": shifted(slab, 1, slabs)}, {"slab": shifted(slab, -1, slabs)}]
+    for d in range(1, near):
+        greeted.append(near_peer(d))
+    for d in range(1, far):
+        greeted.append(far_peer(d))
+    for device in greeted:
+        pl.semaphore_signal(barrier, inc=1, device_id=device, device_id_type=MESH)
 
     def mode_copy(plane):
         return pltpu.make_async_copy(modes_hbm.at[:, plane], modes.at[:, plane], mode_sem.at[plane])
@@ -155,7 +173,7 @@
         return carry
 
     lax.fori_loop(0, count, edges, 0)
-    pl.semaphore_wait(barrier, tiles + slabs - 2)
+    pl.semaphore_wait(barrier, len(greeted))
 
     def faces(step):
         up_x, down_x = {"slab": shifted(slab, 1, slabs)}, {"slab": shifted(slab, -1, slabs)}
@@ -216,22 +234,23 @@
 
         lax.fori_loop(first, last, plane_step, 0)
 
-    def reduce_start(axis, size, sums, send, recv):
-        me = lax.axis_index(axis)
-        return [
+    def reduce_start(size, me, peer_of, sums, send, recv):
+        copies = [
             pltpu.make_async_remote_copy(
                 src_ref=sums.at[0],
                 dst_ref=sums.at[1 + me],
                 send_sem=send.at[d],
                 recv_sem=recv.at[d],
-                device_id={axis: shifted(me, d, size)},
+                device_id=peer_of(d),
                 device_id_type=MESH,
             )
             for d in range(1, size)
         ]
-
-    def reduce_end(axis, size, sums, copies):
-        me = lax.axis_index(axis)
+        for copy in copies:
+            copy.start()
+        return copies
+
+    def reduce_end(size, me, sums, copies):
         sums[1 + me] = sums[0]
         for copy in copies:
             copy.wait()
@@ -239,6 +258,12 @@
         for i in range(1, size):
             total = total + sums[1 + i]
         return total
+
+    def near_start(which, sums):
+        return reduce_start(near, near_me, near_peer, sums, one_send.at[which], one_recv.at[which])
+
+    def far_start(which, sums):
+        return reduce_start(far, far_me, far_peer, sums, two_send.at[which], two_recv.at[which])
 
     first_faces = faces(0)
     for copy in first_faces:
@@ -249,10 +274,6 @@
     products[...] = jnp.zeros_like(products)
     squares[...] = jnp.zeros_like(squares)
     gram_planes(0, planes)
-    sums_one[0] = matched(products[...], RANK)
-    basis_one = reduce_start("tile", tiles, sums_one, one_send.at[0], one_recv.at[0])
-    for copy in basis_one:
-        copy.start()
     for copy in first_faces:
         copy.wait()
 
@@ -266,10 +287,8 @@
     for copy in second_faces:
         copy.start()
     send_strips(1)
-    sums_two[0] = reduce_end("tile", tiles, sums_one, basis_one)
-    basis_two = reduce_start("slab", slabs, sums_two, two_send.at[0], two_recv.at[0])
-    for copy in basis_two:
-        copy.start()
+    sums_one[0] = matched(products[...], RANK)
+    basis_near = near_start(0, sums_one)
     for copy in second_faces:
         copy.wait()
 
@@ -277,31 +296,9 @@
         advanced[c, x] = value.reshape(2, SUB, LANES)
 
     advance_planes(flow.at[1], low.at[1], high.at[1], nu, store_second)
+    sums_two[0] = reduce_end(near, near_me, sums_one, basis_near)
+    basis_far = far_start(0, sums_two)
     send_strips(2)
-
-    weight = weight_row[...]
-    early_row = iota((RANK, LANES), 0)
-    early_lane = iota((RANK, LANES), 1)
-    tall_weight = jnp.broadcast_to(weight, (LANES, LANES)).T[:RANK]
-    early_ref[...] = reduce_end("slab", slabs, sums_two, basis_two) * weight * tall_weight + (
-        early_lane == early_row + 64
-    ).astype(F32)
-
-    def eliminate(i, carry):
-        block = early_ref[...]
-        pivot_row = early_ref[pl.ds(i, 1)]
-        column = jnp.sum(jnp.where(early_lane == i, block, 0.0), axis=1, keepdims=True)
-        pivot = jnp.sum(jnp.where(early_lane[:1] == i, pivot_row, 0.0), axis=1, keepdims=True)
-        update = column * (pivot_row / pivot)
-        early_ref[...] = block - jnp.where(early_row > i, update, 0.0)
-        return carry
-
-    lax.fori_loop(0, RANK, eliminate, 0)
-    eliminated = early_ref[...]
-    pivots = jnp.sum(jnp.where(early_lane == early_row, eliminated, 0.0), axis=1, keepdims=True)
-    eliminated = eliminated / jnp.sqrt(pivots)
-    early_ref[...] = jnp.where((early_lane >= early_row) | (early_lane >= 64), eliminated, 0.0)
-
     snap_rows = 3 * SNAPS * SUB
     products[:snap_rows] = jnp.zeros((snap_rows, WIDE), F32)
 
@@ -356,21 +353,43 @@
     lane = iota((SUB, LANES), 1)
     result = jnp.zeros((SUB, LANES), F32)
     for s in range(SNAPS):
-        line = by_part[3 * s : 3 * s + 1] + by_part[3 * s + 1 : 3 * s + 2] + by_part[3 * s + 2 : 3 * s + 3]
-        result = jnp.where(row == s, line, result)
+        at = 3 * s
+        joined = by_part[at : at + 1] + by_part[at + 1 : at + 2] + by_part[at + 2 : at + 3]
+        result = jnp.where(row == s, joined, result)
     for a in range(SNAPS):
         for b in range(a + 1):
             here = ((row == a) & (lane == RANK + b)) | ((row == b) & (lane == RANK + a))
             result = jnp.where(here, jnp.sum(squares[3 * a + b]), result)
     late_sums_one[0] = result
-    late = reduce_start("tile", tiles, late_sums_one, one_send.at[1], one_recv.at[1])
-    for copy in late:
-        copy.start()
-    late_sums_two[0] = reduce_end("tile", tiles, late_sums_one, late)
-    late = reduce_start("slab", slabs, late_sums_two, two_send.at[1], two_recv.at[1])
-    for copy in late:
-        copy.start()
-    late_ref[...] = reduce_end("slab", slabs, late_sums_two, late)
+    late_near = near_start(1, late_sums_one)
+    weight = weight_row[...]
+    early_row = iota((RANK, LANES), 0)
+    early_lane = iota((RANK, LANES), 1)
+    tall_weight = jnp.broadcast_to(weight, (LANES, LANES)).T[:RANK]
+    early = reduce_end(far, far_me, sums_two, basis_far) * weight * tall_weight
+    early = early + (early_lane == early_row + 64).astype(F32)
+    blocks = [early[SUB * b : SUB * b + SUB] for b in range(RANK // SUB)]
+
+    def eliminate(first, last):
+        for i in range(first, last):
+            at, inner = divmod(i, SUB)
+            pivot_row = blocks[at][inner : inner + 1]
+            scaled = pivot_row / pivot_row[:, i : i + 1]
+            for b in range(at, RANK // SUB):
+                update = blocks[b][:, i : i + 1] * scaled
+                if b == at:
+                    update = jnp.where(row > inner, update, 0.0)
+                blocks[b] = blocks[b] - update
+
+    eliminate(0, RANK // 2)
+    late_sums_two[0] = reduce_end(near, near_me, late_sums_one, late_near)
+    late_far = far_start(1, late_sums_two)
+    eliminate(RANK // 2, RANK)
+    eliminated = jnp.concatenate(blocks, axis=0)
+    pivots = jnp.sum(jnp.where(early_lane == early_row, eliminated, 0.0), axis=1, keepdims=True)
+    eliminated = eliminated / jnp.sqrt(pivots)
+    early_ref[...] = jnp.where((early_lane >= early_row) | (early_lane >= 64), eliminated, 0.0)
+    late_ref[...] = reduce_end(far, far_me, late_sums_two, late_far)
 
     for k in range(SNAPS):
         for d in range(1, tiles):
@@ -530,10 +549,10 @@
             pltpu.VMEM((2, 3, count, LANES), F32),
             pltpu.VMEM((WIDE, WIDE), F32),
             pltpu.VMEM((9, SUB, LANES), F32),
-            pltpu.VMEM((1 + tiles, RANK, LANES), F32),
-            pltpu.VMEM((1 + slabs, RANK, LANES), F32),
-            pltpu.VMEM((1 + tiles, SUB, LANES), F32),
-            pltpu.VMEM((1 + slabs, SUB, LANES), F32),
+            pltpu.VMEM((1 + slabs // HALVES, RANK, LANES), F32),
+            pltpu.VMEM((1 + HALVES * tiles, RANK, LANES), F32),
+            pltpu.VMEM((1 + slabs // HALVES, SUB, LANES), F32),
+            pltpu.VMEM((1 + HALVES * tiles, SUB, LANES), F32),
             pltpu.VMEM((1, LANES), F32),
             pltpu.SemaphoreType.DMA((2,)),
             pltpu.SemaphoreType.DMA((planes,)),
@@ -542,10 +561,10 @@
             pltpu.SemaphoreType.DMA((2, 4)),
             pltpu.SemaphoreType.DMA((SNAPS, tiles)),
             pltpu.SemaphoreType.DMA((SNAPS, tiles)),
-            pltpu.SemaphoreType.DMA((2, tiles)),
-            pltpu.SemaphoreType.DMA((2, tiles)),
-            pltpu.SemaphoreType.DMA((2, slabs)),
-            pltpu.SemaphoreType.DMA((2, slabs)),
+            pltpu.SemaphoreType.DMA((2, slabs // HALVES)),
+            pltpu.SemaphoreType.DMA((2, slabs // HALVES)),
+            pltpu.SemaphoreType.DMA((2, HALVES * tiles)),
+            pltpu.SemaphoreType.DMA((2, HALVES * tiles)),
         ],
         compiler_params=pltpu.CompilerParams(
             collective_id=0, has_side_effects=True, vmem_limit_bytes=EXCHANGE_VMEM

time: 76.7 us -> 71.4 us (0.931)
  Pallas kernels: 75.8 us -> 70.5 us
    pallas_call x1, Pallas kernels: 61.5 us -> 56.2 us  [shards(): pl.pallas_call(functools.partial(exchange_kernel, slabs, tiles), in_specs...]
where the time goes in v4:
time: 71.4 us; the launch traced here: 71.2 us
  Pallas kernels  70.5 us (99%)
    pallas_call x1, Pallas kernels, shards(): pl.pallas_call(functools.partial(exchange_kernel, slabs, tiles), in_specs...  56.2 us
    pallas_call x1, Pallas kernels, shards(): pl.pallas_call(functools.partial(rotate_kernel, row_scale), in_specs=[vme...  14.3 us

profile of v4, /device:TPU:1, one launch (start us, length us, event | category | flops | bytes accessed | tf_op | source)
XLA Modules:
  0.0 71.2 jit_solution(7349788790443507129)
XLA Ops:
  0.6 0.0 copy-start
  0.6 0.0 copy-start.1
  0.7 56.2 %exchange.1 = (f32[3,32,2,8,128]{4,3,2,1,0:T(8,128)S(1)}, f32[32,128]{1,0:T(8,128)S(1)}, f32[8,128]{1,0:T(8,128)S(1)}, f32[3,3,4,16,8,128]{5,4,3,2,1,0:T(8,128)S(1)}) custom-call(f32[3,32,2,8,128]{4,3,2,1,0:T(8,128)} %bitcast.12, f32[32,2,8,128]{3,2,1,0:T(8,128)} %bitcast.13, bf16[32,12,16,8,128]{4,3,2,1,0:T(8,128)(2,1)} %bitcast.10, f32[1,32]{1,0:T(1,128)} %bitcast.8), custom_call_target="tpu_custom_call" | custom-call | tf_op jit(solution)/shard_map/exchange/pallas_call | solution.py:532
  56.9 0.0 copy-done
  56.9 0.0 copy-done.1
  56.9 14.3 %rotate.1 = (f32[3,32,2,8,128]{4,3,2,1,0:T(8,128)}, f32[35,35]{1,0:T(8,128)}, bf16[32,12,16,8,128]{4,3,2,1,0:T(8,128)(2,1)}) custom-call(f32[32,128]{1,0:T(8,128)S(1)} %get-tuple-element.10.early_ref, f32[8,128]{1,0:T(8,128)S(1)} %get-tuple-element.11.late_ref, f32[1,32]{1,0:T(1,128)S(1)} %bitcast.9, f32[32,35]{1,0:T(8,128)S(1)} %bitcast.7, ...), custom_call_target="tpu_custom_call" | custom-call | tf_op jit(solution)/shard_map/rotate/pallas_call | solution.py:574
Async XLA Ops:
  0.6 56.2 %copy-start = (f32[35,32]{0,1:T(8,128)S(1)}, f32[35,32]{0,1:T(8,128)}, u32[]{:S(2)}) copy-start(f32[35,32]{0,1:T(8,128)} %param.9) | copy-start | bytes 13444
  0.6 56.2 %copy-start.1 = (f32[32]{0:T(128)S(1)}, f32[32]{0:T(128)}, u32[]{:S(2)}) copy-start(f32[32]{0:T(128)} %param.8) | copy-start | bytes 388

commit v5 on v4

--- a/solution.py
+++ b/solution.py
@@ -22,8 +22,8 @@
 GRAM_ROWS = 40
 CORES = 2
 HALVES = 2
-EXCHANGE_VMEM = 63_700_000
-ROTATE_VMEM = 50 << 20
+EXCHANGE_VMEM = 25_900_000
+ROTATE_VMEM = 10_000_000
 
 
 def iota(shape, dim):
@@ -51,6 +51,16 @@
     left = ref[(slice(None), *front, tile)].reshape(WIDE, LANES)
     right = ref[(slice(None), *front, tile + 1)].reshape(WIDE, LANES)
     return jnp.concatenate([left, right], axis=1)
+
+
+def spread_weights(values, rows, out_ref):
+    tall_rows = rows * SUB
+    spread = ((iota((LANES, WIDE), 0) - 64) == iota((LANES, WIDE), 1) // SUB).astype(BF16)
+    same = iota((tall_rows, WIDE), 0) % SUB == iota((tall_rows, WIDE), 1) % SUB
+    for part, piece in enumerate(pieces(values, 2)):
+        wide = jnp.dot(piece, spread, preferred_element_type=F32)[:rows]
+        tall = jnp.broadcast_to(wide[:, None, :], (rows, SUB, WIDE)).reshape(tall_rows, WIDE)
+        out_ref[tall_rows * part : tall_rows * part + tall_rows] = jnp.where(same, tall, 0.0).astype(BF16)
 
 
 def advance_planes(padded, low, high, viscosity, store):
@@ -87,15 +97,20 @@
 def exchange_kernel(
     slabs,
     tiles,
+    row_scale,
     vel_hbm,
     nu_hbm,
     modes_hbm,
     sigma_ref,
+    rotation_ref,
     advanced,
     early_ref,
     late_ref,
     snaps,
     modes,
+    partly,
+    rotate_ref,
+    rotation_wide,
     flow,
     nu,
     low,
@@ -252,8 +267,9 @@
 
     def reduce_end(size, me, sums, copies):
         sums[1 + me] = sums[0]
+        sent.extend(copies)
         for copy in copies:
-            copy.wait()
+            copy.wait_recv()
         total = sums[1]
         for i in range(1, size):
             total = total + sums[1 + i]
@@ -265,6 +281,7 @@
     def far_start(which, sums):
         return reduce_start(far, far_me, far_peer, sums, two_send.at[which], two_recv.at[which])
 
+    sent = []
     first_faces = faces(0)
     for copy in first_faces:
         copy.start()
@@ -274,8 +291,9 @@
     products[...] = jnp.zeros_like(products)
     squares[...] = jnp.zeros_like(squares)
     gram_planes(0, planes)
+    sent.extend(first_faces)
     for copy in first_faces:
-        copy.wait()
+        copy.wait_recv()
 
     def store_first(c, x, value):
         flow[1, c, x + 1] = value.reshape(2, SUB, LANES)
@@ -289,8 +307,9 @@
     send_strips(1)
     sums_one[0] = matched(products[...], RANK)
     basis_near = near_start(0, sums_one)
+    sent.extend(second_faces)
     for copy in second_faces:
-        copy.wait()
+        copy.wait_recv()
 
     def store_second(c, x, value):
         advanced[c, x] = value.reshape(2, SUB, LANES)
@@ -346,10 +365,55 @@
 
         lax.fori_loop(0, tiles, piece, 0)
 
-    gram_pieces((0, 1))
-    gram_pieces((2,))
+    row = iota((SUB, LANES), 0)
+    weight = weight_row[...]
+    early_row = iota((RANK, LANES), 0)
+    early_lane = iota((RANK, LANES), 1)
+    tall_weight = jnp.broadcast_to(weight, (LANES, LANES)).T[:RANK]
+    early = reduce_end(far, far_me, sums_two, basis_far) * weight * tall_weight
+    early = early + (early_lane == early_row + 64).astype(F32)
+    blocks = [early[SUB * b : SUB * b + SUB] for b in range(RANK // SUB)]
+
+    def eliminate(first, last):
+        for i in range(first, last):
+            at, inner = divmod(i, SUB)
+            pivot_row = blocks[at][inner : inner + 1]
+            scaled = pivot_row / pivot_row[:, i : i + 1]
+            for b in range(at, RANK // SUB):
+                update = blocks[b][:, i : i + 1] * scaled
+                if b == at:
+                    update = jnp.where(row > inner, update, 0.0)
+                blocks[b] = blocks[b] - update
+
+    eliminate(0, RANK)
+    eliminated = jnp.concatenate(blocks, axis=0)
+    pivots = jnp.sum(jnp.where(early_lane == early_row, eliminated, 0.0), axis=1, keepdims=True)
+    eliminated = eliminated / jnp.sqrt(pivots)
+    early_ref[...] = jnp.where((early_lane >= early_row) | (early_lane >= 64), eliminated, 0.0)
+    inverse_top = jnp.where(early_lane >= 64, eliminated, 0.0)
+    rotation_wide[...] = jnp.zeros_like(rotation_wide)
+    rotation_wide[:, :K] = rotation_ref[...]
+    mixed = row_scale * jnp.dot(
+        rotation_wide[:, :RANK], inverse_top, precision=HIGHEST, preferred_element_type=F32
+    )
+    spread_weights(mixed * pltpu.roll(weight, 64, 1), RANK, rotate_ref)
+
+    def rotate_planes(first, last):
+        def plane_step(plane, carry):
+            for t in range(0, modes.shape[2], 2):
+                both = jnp.dot(
+                    rotate_ref[...], wide_pair(modes, plane, t), preferred_element_type=F32
+                )
+                both = both[:WIDE] + both[WIDE:]
+                for half in range(2):
+                    part = both[:, LANES * half : LANES * half + LANES]
+                    partly[plane, t + half] = part.reshape(RANK, SUB, LANES)
+            return carry
+
+        lax.fori_loop(first, last, plane_step, 0)
+
+    gram_pieces((0, 1, 2))
     by_part = matched(products[:snap_rows], 3 * SNAPS)
-    row = iota((SUB, LANES), 0)
     lane = iota((SUB, LANES), 1)
     result = jnp.zeros((SUB, LANES), F32)
     for s in range(SNAPS):
@@ -362,35 +426,14 @@
             result = jnp.where(here, jnp.sum(squares[3 * a + b]), result)
     late_sums_one[0] = result
     late_near = near_start(1, late_sums_one)
-    weight = weight_row[...]
-    early_row = iota((RANK, LANES), 0)
-    early_lane = iota((RANK, LANES), 1)
-    tall_weight = jnp.broadcast_to(weight, (LANES, LANES)).T[:RANK]
-    early = reduce_end(far, far_me, sums_two, basis_far) * weight * tall_weight
-    early = early + (early_lane == early_row + 64).astype(F32)
-    blocks = [early[SUB * b : SUB * b + SUB] for b in range(RANK // SUB)]
-
-    def eliminate(first, last):
-        for i in range(first, last):
-            at, inner = divmod(i, SUB)
-            pivot_row = blocks[at][inner : inner + 1]
-            scaled = pivot_row / pivot_row[:, i : i + 1]
-            for b in range(at, RANK // SUB):
-                update = blocks[b][:, i : i + 1] * scaled
-                if b == at:
-                    update = jnp.where(row > inner, update, 0.0)
-                blocks[b] = blocks[b] - update
-
-    eliminate(0, RANK // 2)
+    rotate_planes(0, planes // 2)
     late_sums_two[0] = reduce_end(near, near_me, late_sums_one, late_near)
     late_far = far_start(1, late_sums_two)
-    eliminate(RANK // 2, RANK)
-    eliminated = jnp.concatenate(blocks, axis=0)
-    pivots = jnp.sum(jnp.where(early_lane == early_row, eliminated, 0.0), axis=1, keepdims=True)
-    eliminated = eliminated / jnp.sqrt(pivots)
-    early_ref[...] = jnp.where((early_lane >= early_row) | (early_lane >= 64), eliminated, 0.0)
+    rotate_planes(planes // 2, planes)
     late_ref[...] = reduce_end(far, far_me, late_sums_two, late_far)
 
+    for copy in sent:
+        copy.wait_send()
     for k in range(SNAPS):
         for d in range(1, tiles):
             bulk(k, d).wait_send()
@@ -432,13 +475,8 @@
     mixed = row_scale * jnp.dot(
         rotation_ref[:, :GRAM_ROWS], inverse, precision=HIGHEST, preferred_element_type=F32
     )
-    sigma_lane = pltpu.roll(sigma_row, 64, 1)
-    spread = ((iota((LANES, WIDE), 0) - 64) == iota((LANES, WIDE), 1) // SUB).astype(BF16)
-    same = iota((WIDE, WIDE), 0) % SUB == iota((WIDE, WIDE), 1) % SUB
-    for part, values in enumerate(pieces(mixed * sigma_lane, 2)):
-        wide = jnp.dot(values, spread, preferred_element_type=F32)
-        tall = jnp.broadcast_to(wide[:, None, :], (RANK, SUB, WIDE)).reshape(WIDE, WIDE)
-        weight_ref[WIDE * part : WIDE * part + WIDE] = jnp.where(same, tall, 0.0).astype(BF16)
+    removed = jnp.dot(weights, inverse_top, precision=HIGHEST, preferred_element_type=F32)
+    spread_weights(removed * pltpu.roll(sigma_row, 64, 1), SNAPS, weight_ref)
     for s in range(SNAPS):
         column = mixed[:, 64 + RANK + s : 64 + RANK + s + 1]
         snap_ref[s] = jnp.broadcast_to(column[:, :, None], (RANK, SUB, LANES))
@@ -450,13 +488,13 @@
     late_ref,
     sigma_ref,
     rotation_ref,
-    modes_hbm,
+    modes,
+    partly,
     snaps,
     flow,
     advanced,
     factor_ref,
     new_modes,
-    modes,
     sigma_row,
     rotation_wide,
     weight_ref,
@@ -464,15 +502,9 @@
     staged,
     flow_sem,
     out_sem,
-    mode_sem,
 ):
     planes, tiles = modes.shape[1], modes.shape[2]
 
-    def mode_copy(plane):
-        return pltpu.make_async_copy(modes_hbm.at[:, plane], modes.at[:, plane], mode_sem.at[plane])
-
-    for plane in range(planes):
-        mode_copy(plane).start()
     passing = pltpu.make_async_copy(flow, advanced, flow_sem)
     passing.start()
     sigma_row[...] = jnp.zeros_like(sigma_row)
@@ -494,15 +526,15 @@
         def _():
             out_copy(plane - 2, slot).wait()
 
-        mode_copy(plane).wait()
         c, w = lax.div(plane, width), lax.rem(plane, width)
         for t in range(0, tiles, 2):
             both = jnp.dot(weight_ref[...], wide_pair(modes, plane, t), preferred_element_type=F32)
-            both = both[:WIDE] + both[WIDE:]
+            both = both[: SNAPS * SUB] + both[SNAPS * SUB :]
             for half in range(2):
-                value = both[:, LANES * half : LANES * half + LANES].reshape(RANK, SUB, LANES)
+                value = partly[plane, t + half]
                 for s in range(SNAPS):
-                    value = value + snap_ref[s] * snaps[s, c, w, t + half][None]
+                    inside = both[SUB * s : SUB * s + SUB, LANES * half : LANES * half + LANES]
+                    value = value + snap_ref[s] * (snaps[s, c, w, t + half] - inside)[None]
                 staged[slot, :, t + half] = value.astype(BF16)
         out_copy(plane, slot).start()
         return carry
@@ -529,18 +561,21 @@
     modes_hbm = basis.reshape(RANK, planes, deep_tiles, SUB, LANES)
     flow_shape = (3, count, 2, SUB, LANES)
     sigma_row = sigma.reshape(1, RANK)
-    flow, early, late, snaps = pl.pallas_call(
-        functools.partial(exchange_kernel, slabs, tiles),
-        in_specs=[hbm_spec(), hbm_spec(), hbm_spec(), vmem_spec()],
-        out_specs=[vmem_spec()] * 4,
+    flow, early, late, snaps, modes, partly = pl.pallas_call(
+        functools.partial(exchange_kernel, slabs, tiles, row_scale),
+        in_specs=[hbm_spec(), hbm_spec(), hbm_spec(), vmem_spec(), vmem_spec()],
+        out_specs=[vmem_spec()] * 6,
         out_shape=[
             pltpu.VMEM(flow_shape, F32),
             pltpu.VMEM((RANK, LANES), F32),
             pltpu.VMEM((SUB, LANES), F32),
             pltpu.VMEM((SNAPS, parts, width, deep_tiles, SUB, LANES), F32),
+            pltpu.VMEM(modes_hbm.shape, BF16),
+            pltpu.VMEM((planes, deep_tiles, RANK, SUB, LANES), F32),
         ],
         scratch_shapes=[
-            pltpu.VMEM(modes_hbm.shape, BF16),
+            pltpu.VMEM((2 * WIDE, WIDE), BF16),
+            pltpu.VMEM((RANK, LANES), F32),
             pltpu.VMEM((2, 3, count + 2, 2, SUB, LANES), F32),
             pltpu.VMEM((count, 2, SUB, LANES), F32),
             pltpu.VMEM((2, 3, count, LANES), F32),
@@ -570,10 +605,10 @@
             collective_id=0, has_side_effects=True, vmem_limit_bytes=EXCHANGE_VMEM
         ),
         name="exchange",
-    )(velocity.reshape(flow_shape), viscosity.reshape(count, 2, SUB, LANES), modes_hbm, sigma_row)
+    )(velocity.reshape(flow_shape), viscosity.reshape(count, 2, SUB, LANES), modes_hbm, sigma_row, rotation.T)
     advanced, factor, rotated = pl.pallas_call(
         functools.partial(rotate_kernel, row_scale),
-        in_specs=[vmem_spec()] * 4 + [hbm_spec(), vmem_spec(), vmem_spec()],
+        in_specs=[vmem_spec()] * 8,
         out_specs=[hbm_spec(), vmem_spec(), hbm_spec()],
         out_shape=[
             jax.ShapeDtypeStruct(flow_shape, F32),
@@ -581,19 +616,17 @@
             jax.ShapeDtypeStruct(modes_hbm.shape, BF16),
         ],
         scratch_shapes=[
-            pltpu.VMEM(modes_hbm.shape, BF16),
             pltpu.VMEM((1, LANES), F32),
             pltpu.VMEM((RANK, LANES), F32),
-            pltpu.VMEM((2 * WIDE, WIDE), BF16),
+            pltpu.VMEM((2 * SNAPS * SUB, WIDE), BF16),
             pltpu.VMEM((SNAPS, RANK, SUB, LANES), F32),
             pltpu.VMEM((2, RANK, deep_tiles, SUB, LANES), BF16),
             pltpu.SemaphoreType.DMA,
             pltpu.SemaphoreType.DMA((2,)),
-            pltpu.SemaphoreType.DMA((planes,)),
         ],
         compiler_params=pltpu.CompilerParams(vmem_limit_bytes=ROTATE_VMEM),
         name="rotate",
-    )(early, late, sigma_row, rotation.T, modes_hbm, snaps, flow)
+    )(early, late, sigma_row, rotation.T, modes, partly, snaps, flow)
     return (advanced.reshape(velocity.shape), factor, rotated.reshape(basis.shape))
 
 

time: 71.4 us -> 71.7 us (level)
  no operation moved by 1% of the time
where the time goes in v5:
time: 71.7 us; the launch traced here: 71 us
  Pallas kernels  70.3 us (98%)
    pallas_call x1, Pallas kernels, shards(): pl.pallas_call(functools.partial(exchange_kernel, slabs, tiles, row_scale...  55.8 us
    pallas_call x1, Pallas kernels, shards(): pl.pallas_call(functools.partial(rotate_kernel, row_scale), in_specs=[vme...  14.4 us

profile of v5, /device:TPU:1, one launch (start us, length us, event | category | flops | bytes accessed | tf_op | source)
XLA Modules:
  0.0 71.0 jit_solution(14773249673391506893)
XLA Ops:
  0.6 0.0 copy-start
  0.6 0.0 copy-start.1
  0.7 55.8 %exchange.1 = (f32[3,32,2,8,128]{4,3,2,1,0:T(8,128)S(1)}, f32[32,128]{1,0:T(8,128)S(1)}, f32[8,128]{1,0:T(8,128)S(1)}, f32[3,3,4,16,8,128]{5,4,3,2,1,0:T(8,128)S...) custom-call(f32[3,32,2,8,128]{4,3,2,1,0:T(8,128)} %bitcast.12, ...), custom_call_target="tpu_custom_call" | custom-call | tf_op jit(solution)/shard_map/exchange/pallas_call | solution.py:564
  56.5 0.0 copy-done
  56.5 0.0 copy-done.1
  56.5 14.4 %rotate.1 = (f32[3,32,2,8,128]{4,3,2,1,0:T(8,128)}, f32[35,35]{1,0:T(8,128)}, bf16[32,12,16,8,128]{4,3,2,1,0:T(8,128)(2,1)}) custom-call(f32[32,128]{1,0:T(8,128)S(1)} %get-tuple-element.12.early_ref, f32[8,128]{1,0:T(8,128)S(1)} %get-tuple-element.13.late_ref, f32[1,32]{1,0:T(1,128)S(1)} %bitcast.10, f32[32,35]{1,0:T(8,128)S(1)} %bitcast.8, ...), custom_call_target="tpu_custom_call" | custom-call | tf_op jit(solution)/shard_map/rotate/pallas_call | solution.py:609
Async XLA Ops:
  0.6 55.9 %copy-start = (f32[35,32]{0,1:T(8,128)S(1)}, f32[35,32]{0,1:T(8,128)}, u32[]{:S(2)}) copy-start(f32[35,32]{0,1:T(8,128)} %param.9) | copy-start | bytes 13444
  0.6 55.9 %copy-start.1 = (f32[32]{0:T(128)S(1)}, f32[32]{0:T(128)}, u32[]{:S(2)}) copy-start(f32[32]{0:T(128)} %param.8) | copy-start | bytes 388

commit v6 on v5

--- a/solution.py
+++ b/solution.py
@@ -477,9 +477,16 @@
     )
     removed = jnp.dot(weights, inverse_top, precision=HIGHEST, preferred_element_type=F32)
     spread_weights(removed * pltpu.roll(sigma_row, 64, 1), SNAPS, weight_ref)
-    for s in range(SNAPS):
-        column = mixed[:, 64 + RANK + s : 64 + RANK + s + 1]
-        snap_ref[s] = jnp.broadcast_to(column[:, :, None], (RANK, SUB, LANES))
+    column = iota((LANES, LANES), 1)
+    picks = (iota((LANES, LANES), 0) - 64 - RANK) == lax.rem(column, SNAPS * SUB) // SUB
+    high_part, low_part = pieces(mixed, 2)
+    first = (picks & (column < 2 * SNAPS * SUB)).astype(BF16)
+    second = (picks & (column >= 2 * SNAPS * SUB) & (column < 3 * SNAPS * SUB)).astype(BF16)
+    wide = jnp.dot(high_part, first, preferred_element_type=F32)
+    wide = wide + jnp.dot(low_part, second, preferred_element_type=F32)
+    tall = jnp.broadcast_to(wide[:, None, :], (RANK, SUB, LANES)).reshape(WIDE, LANES)
+    same = iota((WIDE, LANES), 0) % SUB == iota((WIDE, LANES), 1) % SUB
+    snap_ref[...] = jnp.where(same, tall, 0.0).astype(BF16)
 
 
 def rotate_kernel(
@@ -530,12 +537,18 @@
         for t in range(0, tiles, 2):
             both = jnp.dot(weight_ref[...], wide_pair(modes, plane, t), preferred_element_type=F32)
             both = both[: SNAPS * SUB] + both[SNAPS * SUB :]
+            flows = [
+                jnp.concatenate([snaps[s, c, w, t], snaps[s, c, w, t + 1]], axis=1)
+                for s in range(SNAPS)
+            ]
+            rest = jnp.concatenate(flows, axis=0) - both
+            coarse = rest.astype(BF16).astype(F32)
+            empty = jnp.zeros((LANES - 3 * SNAPS * SUB, 2 * LANES), F32)
+            stack = jnp.concatenate([coarse, rest - coarse, coarse, empty], axis=0).astype(BF16)
+            added = jnp.dot(snap_ref[...], stack, preferred_element_type=F32)
             for half in range(2):
-                value = partly[plane, t + half]
-                for s in range(SNAPS):
-                    inside = both[SUB * s : SUB * s + SUB, LANES * half : LANES * half + LANES]
-                    value = value + snap_ref[s] * (snaps[s, c, w, t + half] - inside)[None]
-                staged[slot, :, t + half] = value.astype(BF16)
+                part = added[:, LANES * half : LANES * half + LANES].reshape(RANK, SUB, LANES)
+                staged[slot, :, t + half] = (partly[plane, t + half] + part).astype(BF16)
         out_copy(plane, slot).start()
         return carry
 
@@ -619,7 +632,7 @@
             pltpu.VMEM((1, LANES), F32),
             pltpu.VMEM((RANK, LANES), F32),
             pltpu.VMEM((2 * SNAPS * SUB, WIDE), BF16),
-            pltpu.VMEM((SNAPS, RANK, SUB, LANES), F32),
+            pltpu.VMEM((WIDE, LANES), BF16),
             pltpu.VMEM((2, RANK, deep_tiles, SUB, LANES), BF16),
             pltpu.SemaphoreType.DMA,
             pltpu.SemaphoreType.DMA((2,)),

time: 71.7 us -> 72.6 us (1.013)
  Pallas kernels: 70.3 us -> 71.1 us
    pallas_call x1, Pallas kernels: 14.4 us -> 15.3 us  [shards(): pl.pallas_call(functools.partial(rotate_kernel, row_scale), in_specs=[vme...]
where the time goes in v6:
time: 72.6 us; the launch traced here: 71.8 us
  Pallas kernels  71.1 us (98%)
    pallas_call x1, Pallas kernels, shards(): pl.pallas_call(functools.partial(exchange_kernel, slabs, tiles, row_scale...  55.8 us
    pallas_call x1, Pallas kernels, shards(): pl.pallas_call(functools.partial(rotate_kernel, row_scale), in_specs=[vme...  15.3 us

profile of v6, /device:TPU:1, one launch (start us, length us, event | category | flops | bytes accessed | tf_op | source)
XLA Modules:
  0.0 71.8 jit_solution(13751729084484697119)
XLA Ops:
  0.6 0.0 copy-start
  0.6 0.0 copy-start.1
  0.7 55.8 %exchange.1 = (f32[3,32,2,8,128]{4,3,2,1,0:T(8,128)S(1)}, f32[32,128]{1,0:T(8,128)S(1)}, f32[8,128]{1,0:T(8,128)S(1)}, f32[3,3,4,16,8,128]{5,4,3,2,1,0:T(8,128)S...) custom-call(f32[3,32,2,8,128]{4,3,2,1,0:T(8,128)} %bitcast.12, ...), custom_call_target="tpu_custom_call" | custom-call | tf_op jit(solution)/shard_map/exchange/pallas_call | solution.py:577
  56.5 0.0 copy-done
  56.5 0.0 copy-done.1
  56.5 15.3 %rotate.1 = (f32[3,32,2,8,128]{4,3,2,1,0:T(8,128)}, f32[35,35]{1,0:T(8,128)}, bf16[32,12,16,8,128]{4,3,2,1,0:T(8,128)(2,1)}) custom-call(f32[32,128]{1,0:T(8,128)S(1)} %get-tuple-element.12.early_ref, f32[8,128]{1,0:T(8,128)S(1)} %get-tuple-element.13.late_ref, f32[1,32]{1,0:T(1,128)S(1)} %bitcast.10, f32[32,35]{1,0:T(8,128)S(1)} %bitcast.8, ...), custom_call_target="tpu_custom_call" | custom-call | tf_op jit(solution)/shard_map/rotate/pallas_call | solution.py:622
Async XLA Ops:
  0.6 55.9 %copy-start = (f32[35,32]{0,1:T(8,128)S(1)}, f32[35,32]{0,1:T(8,128)}, u32[]{:S(2)}) copy-start(f32[35,32]{0,1:T(8,128)} %param.9) | copy-start | bytes 13444
  0.6 55.9 %copy-start.1 = (f32[32]{0:T(128)S(1)}, f32[32]{0:T(128)}, u32[]{:S(2)}) copy-start(f32[32]{0:T(128)} %param.8) | copy-start | bytes 388

commit v7 on v4

--- a/solution.py
+++ b/solution.py
@@ -252,8 +252,9 @@
 
     def reduce_end(size, me, sums, copies):
         sums[1 + me] = sums[0]
+        sent.extend(copies)
         for copy in copies:
-            copy.wait()
+            copy.wait_recv()
         total = sums[1]
         for i in range(1, size):
             total = total + sums[1 + i]
@@ -265,6 +266,7 @@
     def far_start(which, sums):
         return reduce_start(far, far_me, far_peer, sums, two_send.at[which], two_recv.at[which])
 
+    sent = []
     first_faces = faces(0)
     for copy in first_faces:
         copy.start()
@@ -274,8 +276,9 @@
     products[...] = jnp.zeros_like(products)
     squares[...] = jnp.zeros_like(squares)
     gram_planes(0, planes)
+    sent.extend(first_faces)
     for copy in first_faces:
-        copy.wait()
+        copy.wait_recv()
 
     def store_first(c, x, value):
         flow[1, c, x + 1] = value.reshape(2, SUB, LANES)
@@ -289,8 +292,9 @@
     send_strips(1)
     sums_one[0] = matched(products[...], RANK)
     basis_near = near_start(0, sums_one)
+    sent.extend(second_faces)
     for copy in second_faces:
-        copy.wait()
+        copy.wait_recv()
 
     def store_second(c, x, value):
         advanced[c, x] = value.reshape(2, SUB, LANES)
@@ -346,8 +350,28 @@
 
         lax.fori_loop(0, tiles, piece, 0)
 
-    gram_pieces((0, 1))
-    gram_pieces((2,))
+    row = iota((SUB, LANES), 0)
+    weight = weight_row[...]
+    early_row = iota((RANK, LANES), 0)
+    early_lane = iota((RANK, LANES), 1)
+    tall_weight = jnp.broadcast_to(weight, (LANES, LANES)).T[:RANK]
+    early = reduce_end(far, far_me, sums_two, basis_far) * weight * tall_weight
+    early = early + (early_lane == early_row + 64).astype(F32)
+    blocks = [early[SUB * b : SUB * b + SUB] for b in range(RANK // SUB)]
+
+    def eliminate(first, last):
+        for i in range(first, last):
+            at, inner = divmod(i, SUB)
+            pivot_row = blocks[at][inner : inner + 1]
+            scaled = pivot_row / pivot_row[:, i : i + 1]
+            for b in range(at, RANK // SUB):
+                update = blocks[b][:, i : i + 1] * scaled
+                if b == at:
+                    update = jnp.where(row > inner, update, 0.0)
+                blocks[b] = blocks[b] - update
+
+    eliminate(0, RANK)
+    gram_pieces((0, 1, 2))
     by_part = matched(products[:snap_rows], 3 * SNAPS)
     row = iota((SUB, LANES), 0)
     lane = iota((SUB, LANES), 1)
@@ -362,35 +386,16 @@
             result = jnp.where(here, jnp.sum(squares[3 * a + b]), result)
     late_sums_one[0] = result
     late_near = near_start(1, late_sums_one)
-    weight = weight_row[...]
-    early_row = iota((RANK, LANES), 0)
-    early_lane = iota((RANK, LANES), 1)
-    tall_weight = jnp.broadcast_to(weight, (LANES, LANES)).T[:RANK]
-    early = reduce_end(far, far_me, sums_two, basis_far) * weight * tall_weight
-    early = early + (early_lane == early_row + 64).astype(F32)
-    blocks = [early[SUB * b : SUB * b + SUB] for b in range(RANK // SUB)]
-
-    def eliminate(first, last):
-        for i in range(first, last):
-            at, inner = divmod(i, SUB)
-            pivot_row = blocks[at][inner : inner + 1]
-            scaled = pivot_row / pivot_row[:, i : i + 1]
-            for b in range(at, RANK // SUB):
-                update = blocks[b][:, i : i + 1] * scaled
-                if b == at:
-                    update = jnp.where(row > inner, update, 0.0)
-                blocks[b] = blocks[b] - update
-
-    eliminate(0, RANK // 2)
     late_sums_two[0] = reduce_end(near, near_me, late_sums_one, late_near)
     late_far = far_start(1, late_sums_two)
-    eliminate(RANK // 2, RANK)
     eliminated = jnp.concatenate(blocks, axis=0)
     pivots = jnp.sum(jnp.where(early_lane == early_row, eliminated, 0.0), axis=1, keepdims=True)
     eliminated = eliminated / jnp.sqrt(pivots)
     early_ref[...] = jnp.where((early_lane >= early_row) | (early_lane >= 64), eliminated, 0.0)
     late_ref[...] = reduce_end(far, far_me, late_sums_two, late_far)
 
+    for copy in sent:
+        copy.wait_send()
     for k in range(SNAPS):
         for d in range(1, tiles):
             bulk(k, d).wait_send()
@@ -488,11 +493,11 @@
         return pltpu.make_async_copy(staged.at[slot], new_modes.at[:, plane], out_sem.at[slot])
 
     def plane_step(plane, carry):
-        slot = lax.rem(plane, 2)
-
-        @pl.when(plane >= 2)
+        slot = lax.rem(plane, 4)
+
+        @pl.when(plane >= 4)
         def _():
-            out_copy(plane - 2, slot).wait()
+            out_copy(plane - 4, slot).wait()
 
         mode_copy(plane).wait()
         c, w = lax.div(plane, width), lax.rem(plane, width)
@@ -508,8 +513,8 @@
         return carry
 
     lax.fori_loop(0, planes, plane_step, 0)
-    for plane in (planes - 2, planes - 1):
-        out_copy(plane, plane % 2).wait()
+    for plane in range(planes - 4, planes):
+        out_copy(plane, plane % 4).wait()
     passing.wait()
 
 
@@ -586,9 +591,9 @@
             pltpu.VMEM((RANK, LANES), F32),
             pltpu.VMEM((2 * WIDE, WIDE), BF16),
             pltpu.VMEM((SNAPS, RANK, SUB, LANES), F32),
-            pltpu.VMEM((2, RANK, deep_tiles, SUB, LANES), BF16),
+            pltpu.VMEM((4, RANK, deep_tiles, SUB, LANES), BF16),
             pltpu.SemaphoreType.DMA,
-            pltpu.SemaphoreType.DMA((2,)),
+            pltpu.SemaphoreType.DMA((4,)),
             pltpu.SemaphoreType.DMA((planes,)),
         ],
         compiler_params=pltpu.CompilerParams(vmem_limit_bytes=ROTATE_VMEM),

time: 71.4 us -> 70.6 us (0.989)
  Pallas kernels: 70.5 us -> 69.7 us
where the time goes in v7:
time: 70.6 us; the launch traced here: 70.4 us
  Pallas kernels  69.7 us (99%)
    pallas_call x1, Pallas kernels, shards(): pl.pallas_call(functools.partial(exchange_kernel, slabs, tiles), in_specs...  55.7 us
    pallas_call x1, Pallas kernels, shards(): pl.pallas_call(functools.partial(rotate_kernel, row_scale), in_specs=[vme...  14 us

profile of v7, /device:TPU:1, one launch (start us, length us, event | category | flops | bytes accessed | tf_op | source)
XLA Modules:
  0.0 70.4 jit_solution(3599204975985038164)
XLA Ops:
  0.6 0.0 copy-start
  0.6 0.0 copy-start.1
  0.7 55.7 %exchange.1 = (f32[3,32,2,8,128]{4,3,2,1,0:T(8,128)S(1)}, f32[32,128]{1,0:T(8,128)S(1)}, f32[8,128]{1,0:T(8,128)S(1)}, f32[3,3,4,16,8,128]{5,4,3,2,1,0:T(8,128)S(1)}) custom-call(f32[3,32,2,8,128]{4,3,2,1,0:T(8,128)} %bitcast.12, f32[32,2,8,128]{3,2,1,0:T(8,128)} %bitcast.13, bf16[32,12,16,8,128]{4,3,2,1,0:T(8,128)(2,1)} %bitcast.10, f32[1,32]{1,0:T(1,128)} %bitcast.8), custom_call_target="tpu_custom_call" | custom-call | tf_op jit(solution)/shard_map/exchange/pallas_call | solution.py:537
  56.4 0.0 copy-done
  56.4 0.0 copy-done.1
  56.4 14.0 %rotate.1 = (f32[3,32,2,8,128]{4,3,2,1,0:T(8,128)}, f32[35,35]{1,0:T(8,128)}, bf16[32,12,16,8,128]{4,3,2,1,0:T(8,128)(2,1)}) custom-call(f32[32,128]{1,0:T(8,128)S(1)} %get-tuple-element.10.early_ref, f32[8,128]{1,0:T(8,128)S(1)} %get-tuple-element.11.late_ref, f32[1,32]{1,0:T(1,128)S(1)} %bitcast.9, f32[32,35]{1,0:T(8,128)S(1)} %bitcast.7, ...), custom_call_target="tpu_custom_call" | custom-call | tf_op jit(solution)/shard_map/rotate/pallas_call | solution.py:579
Async XLA Ops:
  0.6 55.8 %copy-start = (f32[35,32]{0,1:T(8,128)S(1)}, f32[35,32]{0,1:T(8,128)}, u32[]{:S(2)}) copy-start(f32[35,32]{0,1:T(8,128)} %param.9) | copy-start | bytes 13444
  0.6 55.8 %copy-start.1 = (f32[32]{0:T(128)S(1)}, f32[32]{0:T(128)}, u32[]{:S(2)}) copy-start(f32[32]{0:T(128)} %param.8) | copy-start | bytes 388
